TPU v7x, 32 devices: a whole 2x2x4 slice. The times are simulated.
32 devices in a mesh: dp: 8 (over z, x), tensor: 4 (over y, core).
Axes of the slice: x: 2, y: 2, z: 4, core: 2. Of those that a mesh axis runs over, the one named last changes fastest.
Arguments:
- inputs: bfloat16 [16, 1024, 768], P('dp'), may hold values from -6 to 6
- cotangent: bfloat16 [16, 1024, 768], P('dp'), may hold values from -6 to 6
- lengths: int32 [16], P('dp'), may hold values from 256 to 1024, as said below
- norm_gain: float32 [768], replicated, may hold values from 0.5 to 1.5
- norm_bias: float32 [768], replicated, may hold values from -2 to 2
- value_weight: bfloat16 [768, 3072], P('dp', 'tensor'), may hold values from -0.21875 to 0.21875
- value_bias: float32 [3072], P('tensor'), may hold values from -2 to 2
- feed_weight: bfloat16 [768, 1536], P('dp', 'tensor'), may hold values from -0.21875 to 0.21875
- feed_bias: float32 [1536], P('tensor'), may hold values from -2 to 2
- mix_forward: bfloat16 [1536, 3072], P('tensor', 'dp'), may hold values from -0.15625 to 0.15625
- mix_backward: bfloat16 [1536, 3072], P('tensor', 'dp'), may hold values from -0.15625 to 0.15625
- mix_bias: float32 [3072], P('tensor'), may hold values from -2 to 2
- out_weight: bfloat16 [3072, 768], P('tensor', 'dp'), may hold values from -0.21875 to 0.21875
- out_bias: float32 [768], replicated, may hold values from -2 to 2
- state_delta: float32 [2, 1536], P(None, 'tensor'), may hold values from -6 to -3
- state_rate: float32 [2, 1536, 64], P(None, 'tensor'), may hold values from 0.1 to 1
- state_readout: float32 [2, 1536, 64], P(None, 'tensor'), may hold values from -0.6 to 0.6
- state_skip: float32 [2, 1536], P(None, 'tensor'), may hold values from -3 to 3
Outputs:
- layer_out: bfloat16 [16, 1024, 768], P('dp')
- input_grad: bfloat16 [16, 1024, 768], P('dp')
- grad_norm_gain: float32 [768], replicated
- grad_norm_bias: float32 [768], replicated
- grad_value_weight: float32 [768, 3072], P('dp', 'tensor')
- grad_value_bias: float32 [3072], P('tensor')
- grad_feed_weight: float32 [768, 1536], P('dp', 'tensor')
- grad_feed_bias: float32 [1536], P('tensor')
- grad_mix_forward: float32 [1536, 3072], P('tensor', 'dp')
- grad_mix_backward: float32 [1536, 3072], P('tensor', 'dp')
- grad_mix_bias: float32 [3072], P('tensor')
- grad_out_weight: float32 [3072, 768], P('tensor', 'dp')
- grad_out_bias: float32 [768], replicated
- grad_state_delta: float32 [2, 1536], P(None, 'tensor')
- grad_state_rate: float32 [2, 1536, 64], P(None, 'tensor')
- grad_state_readout: float32 [2, 1536, 64], P(None, 'tensor')
- grad_state_skip: float32 [2, 1536], P(None, 'tensor')
Inputs may be any that keep to these rules, and one draw needn't show every extreme that they name: `lengths`: each slot's number of valid positions; every draw has a slot of exactly 1024.
All inputs are finite; a program needn't handle non-finite values.
Results may differ from a plain program's by a relative error of at most 0.0067.
Values may be sent and summed in bfloat16 or wider, within the bound.
No kernel may reach another device: no remote copies, remote signals or barrier semaphores. Data moves between devices by JAX's collectives and lax.ppermute only.
A program may use at most 448 MiB of HBM per device.

v0:
```python
import jax
import jax.numpy as jnp
from jax import lax
from jax.sharding import PartitionSpec as P

MB = 2


EPSILON = 1e-05
PRECISE = lax.Precision.HIGHEST


def layer_norm(rows, norm_gain, norm_bias):
    center = rows - jnp.mean(rows, axis=-1, keepdims=True)
    spread = jnp.mean(center * center, axis=-1, keepdims=True)
    return center * lax.rsqrt(spread + EPSILON) * norm_gain + norm_bias


def causal_scan(signal, log_step, decay_rate, readout, skip_gain):
    slot_count, length, channels = signal.shape
    window = min(128, length)
    blocks = length // window
    step_size = jnp.exp(log_step)
    decay_step = step_size[:, None] * decay_rate
    weights = readout * step_size[:, None]
    offsets = jnp.arange(window, dtype=jnp.float32)
    powers = jnp.exp(-decay_step[:, :, None] * offsets)
    kernel = jnp.einsum("hn,hnk->hk", weights, powers, precision=PRECISE)
    lag_index = jnp.arange(window)[:, None] - jnp.arange(window)[None, :]
    toeplitz = jnp.where(lag_index >= 0, kernel[:, jnp.maximum(lag_index, 0)], 0.0)
    pieces = signal.reshape(slot_count, blocks, window, channels)
    inside = jnp.einsum("hts,absh->abth", toeplitz, pieces, precision=PRECISE)
    closing = jnp.exp(-decay_step[:, :, None] * (window - 1.0 - offsets))
    summary = jnp.einsum("hns,absh->abhn", closing, pieces, precision=PRECISE)
    block_decay = jnp.exp(-decay_step * window)

    def advance(carried, update):
        return (block_decay * carried + update, carried)

    initial = jnp.zeros((slot_count, channels, decay_step.shape[1]), jnp.float32)
    _, before = lax.scan(advance, initial, jnp.moveaxis(summary, 1, 0))
    opening = weights[:, :, None] * jnp.exp(-decay_step[:, :, None] * (offsets + 1.0))
    outside = jnp.einsum("hnt,bahn->abth", opening, before, precision=PRECISE)
    return (inside + outside).reshape(slot_count, length, channels) + skip_gain * signal


def reverse_scan(signal, log_step, decay_rate, readout, skip_gain):
    return jnp.flip(causal_scan(jnp.flip(signal, 1), log_step, decay_rate, readout, skip_gain), 1)


def shards(
    inputs,
    cotangent,
    lengths,
    norm_gain,
    norm_bias,
    value_weight,
    value_bias,
    feed_weight,
    feed_bias,
    mix_forward,
    mix_backward,
    mix_bias,
    out_weight,
    out_bias,
    state_delta,
    state_rate,
    state_readout,
    state_skip,
):
    slots_local, length, model_width = inputs.shape
    slots_micro = slots_local // MB
    tokens_micro = slots_micro * length
    weights_local = (value_weight, feed_weight, mix_forward, mix_backward, out_weight)
    shard_totals = tuple((jnp.zeros(matrix.shape, jnp.float32) for matrix in weights_local))
    small_totals = shard_totals
    layer_rows = []
    input_rows = []
    for micro_batch in range(MB):
        chosen = slice(micro_batch * slots_micro, (micro_batch + 1) * slots_micro)
        rows_in = inputs[chosen].astype(jnp.float32)
        live_mask = (jnp.arange(length)[None, :] < lengths[chosen][:, None]).astype(jnp.float32)[
            :, :, None
        ]
        flat_mask = live_mask.reshape(tokens_micro, 1)
        gathered = (
            lax.all_gather(value_weight, "dp", axis=0, tiled=True),
            lax.all_gather(feed_weight, "dp", axis=0, tiled=True),
            lax.all_gather(mix_forward, "dp", axis=1, tiled=True),
            lax.all_gather(mix_backward, "dp", axis=1, tiled=True),
            lax.all_gather(out_weight, "dp", axis=1, tiled=True),
        )
        value_full, feed_full, forward_full, backward_full, output_full = gathered
        normed, norm_pull = jax.vjp(layer_norm, rows_in, norm_gain, norm_bias)
        normed_low = normed.astype(jnp.bfloat16).reshape(tokens_micro, model_width)
        value_pre = jnp.dot(normed_low, value_full, preferred_element_type=jnp.float32) + value_bias
        value_act, value_pull = jax.vjp(jax.nn.gelu, value_pre)
        feed_pre = jnp.dot(normed_low, feed_full, preferred_element_type=jnp.float32) + feed_bias

        def feed_gate(pre_values):
            return jax.nn.gelu(pre_values).reshape(slots_micro, length, -1) * live_mask

        signal, feed_pull = jax.vjp(feed_gate, feed_pre)
        ahead_scan, ahead_pull = jax.vjp(
            causal_scan, signal, state_delta[0], state_rate[0], state_readout[0], state_skip[0]
        )
        behind, behind_pull = jax.vjp(
            reverse_scan, signal, state_delta[1], state_rate[1], state_readout[1], state_skip[1]
        )
        ahead_low = ahead_scan.astype(jnp.bfloat16).reshape(tokens_micro, -1)
        behind_low = behind.astype(jnp.bfloat16).reshape(tokens_micro, -1)
        mixed_part = jnp.dot(ahead_low, forward_full, preferred_element_type=jnp.float32) + jnp.dot(
            behind_low, backward_full, preferred_element_type=jnp.float32
        )
        mixed_sum = (
            lax.psum_scatter(mixed_part, "tensor", scatter_dimension=1, tiled=True) + mix_bias
        )
        gate_act, gate_pull = jax.vjp(jax.nn.gelu, mixed_sum)
        hidden = (gate_act * value_act).astype(jnp.bfloat16)
        branch = lax.psum(
            jnp.dot(hidden, output_full, preferred_element_type=jnp.float32), "tensor"
        )
        layer_flat = flat_mask * (rows_in.reshape(tokens_micro, model_width) + branch + out_bias)
        layer_rows.append(layer_flat.astype(jnp.bfloat16).reshape(slots_micro, length, model_width))
        value_back, feed_back, forward_back, backward_back, output_back = (
            lax.all_gather(value_weight, "dp", axis=0, tiled=True),
            lax.all_gather(feed_weight, "dp", axis=0, tiled=True),
            lax.all_gather(mix_forward, "dp", axis=1, tiled=True),
            lax.all_gather(mix_backward, "dp", axis=1, tiled=True),
            lax.all_gather(out_weight, "dp", axis=1, tiled=True),
        )
        upstream = (
            cotangent[chosen].reshape(tokens_micro, model_width).astype(jnp.float32) * flat_mask
        )
        upstream_low = upstream.astype(jnp.bfloat16)
        grad_out_w = jnp.einsum(
            "tk,td->kd", hidden, upstream_low, preferred_element_type=jnp.float32
        )
        grad_hidden = jnp.einsum(
            "td,kd->tk", upstream_low, output_back, preferred_element_type=jnp.float32
        )
        grad_gate = gate_pull(grad_hidden * value_act)[0].astype(jnp.bfloat16)
        grad_value = value_pull(grad_hidden * gate_act)[0].astype(jnp.bfloat16)
        grad_value_w = jnp.einsum(
            "td,tk->dk", normed_low, grad_value, preferred_element_type=jnp.float32
        )
        features = jnp.einsum(
            "tk,dk->td", grad_value, value_back, preferred_element_type=jnp.float32
        )
        column_piece = lax.all_gather(grad_gate, "tensor", axis=1, tiled=True)
        grad_ahead = jnp.einsum(
            "tk,ck->tc", column_piece, forward_back, preferred_element_type=jnp.float32
        )
        grad_behind = jnp.einsum(
            "tk,ck->tc", column_piece, backward_back, preferred_element_type=jnp.float32
        )
        forward_piece = jnp.einsum(
            "tc,tk->ck", ahead_low, column_piece, preferred_element_type=jnp.float32
        )
        backward_piece = jnp.einsum(
            "tc,tk->ck", behind_low, column_piece, preferred_element_type=jnp.float32
        )
        grad_fwd_w = forward_piece
        grad_bwd_w = backward_piece
        grad_ahead, grad_behind, grad_fwd_w, grad_bwd_w = (
            grad_ahead,
            grad_behind,
            grad_fwd_w,
            grad_bwd_w,
        )
        ahead_grads = ahead_pull(grad_ahead.reshape(slots_micro, length, -1))
        behind_grads = behind_pull(grad_behind.reshape(slots_micro, length, -1))
        grad_feed = feed_pull(ahead_grads[0] + behind_grads[0])[0].astype(jnp.bfloat16)
        grad_feed_w = jnp.einsum(
            "td,tk->dk", normed_low, grad_feed, preferred_element_type=jnp.float32
        )
        features = features + jnp.einsum(
            "tk,dk->td", grad_feed, feed_back, preferred_element_type=jnp.float32
        )
        features = lax.psum(features, "tensor")
        grad_rows, grad_gain, grad_bias = norm_pull(
            features.reshape(slots_micro, length, model_width)
        )
        input_flat = grad_rows.reshape(tokens_micro, model_width) + upstream
        input_rows.append(input_flat.astype(jnp.bfloat16).reshape(slots_micro, length, model_width))
        small_now = (
            grad_gain,
            grad_bias,
            jnp.sum(grad_value.astype(jnp.float32), axis=0),
            jnp.sum(grad_feed.astype(jnp.float32), axis=0),
            jnp.sum(grad_gate.astype(jnp.float32), axis=0),
            jnp.sum(upstream, axis=0),
            jnp.stack([ahead_grads[1], behind_grads[1]]),
            jnp.stack([ahead_grads[2], behind_grads[2]]),
            jnp.stack([ahead_grads[3], behind_grads[3]]),
            jnp.stack([ahead_grads[4], behind_grads[4]]),
        )
        if micro_batch == 0:
            small_totals = small_now
        else:
            small_totals = jax.tree.map(jnp.add, small_totals, small_now)
        grad_tuple = (grad_value_w, grad_feed_w, grad_fwd_w, grad_bwd_w, grad_out_w)
        reduced = (
            lax.psum_scatter(grad_tuple[0], "dp", scatter_dimension=0, tiled=True),
            lax.psum_scatter(grad_tuple[1], "dp", scatter_dimension=0, tiled=True),
            lax.psum_scatter(grad_tuple[2], "dp", scatter_dimension=1, tiled=True),
            lax.psum_scatter(grad_tuple[3], "dp", scatter_dimension=1, tiled=True),
            lax.psum_scatter(grad_tuple[4], "dp", scatter_dimension=1, tiled=True),
        )
        shard_totals = tuple((total + part_sum for total, part_sum in zip(shard_totals, reduced)))
    small_sums = lax.psum(small_totals, "dp")
    layer_out = jnp.concatenate(layer_rows, axis=0)
    input_grad = jnp.concatenate(input_rows, axis=0)
    return (
        layer_out,
        input_grad,
        small_sums[0],
        small_sums[1],
        shard_totals[0],
        small_sums[2],
        shard_totals[1],
        small_sums[3],
        shard_totals[2],
        shard_totals[3],
        small_sums[4],
        shard_totals[4],
        small_sums[5],
        small_sums[6],
        small_sums[7],
        small_sums[8],
        small_sums[9],
    )


def solution(mesh):
    placed = (
        P("dp", None, None),
        P("dp", None, None),
        P("dp"),
        P(),
        P(),
        P("dp", "tensor"),
        P("tensor"),
        P("dp", "tensor"),
        P("tensor"),
        P("tensor", "dp"),
        P("tensor", "dp"),
        P("tensor"),
        P("tensor", "dp"),
        P(),
        P(None, "tensor"),
        P(None, "tensor", None),
        P(None, "tensor", None),
        P(None, "tensor"),
    )
    return jax.shard_map(
        shards,
        mesh=mesh,
        in_specs=placed,
        out_specs=(
            P("dp", None, None),
            P("dp", None, None),
            P(),
            P(),
            P("dp", "tensor"),
            P("tensor"),
            P("dp", "tensor"),
            P("tensor"),
            P("tensor", "dp"),
            P("tensor", "dp"),
            P("tensor"),
            P("tensor", "dp"),
            P(),
            P(None, "tensor"),
            P(None, "tensor", None),
            P(None, "tensor", None),
            P(None, "tensor"),
        ),
        check_vma=False,
    )
```

profile of v0, /device:TPU:0, one launch (start us, length us, event | category | flops | bytes accessed | tf_op | source)
XLA Modules:
  0.0 3271.2 jit_solution(15581725082988454988)
XLA Ops:
  26.3 35.3 %all_gather.14 = bf16[768,384]{1,0:T(8,128)(2,1)S(1)} all-gather(bf16[96,384]{1,0:T(8,128)(2,1)S(1)} %copy-done.123), channel_id=1, replica_groups=mesh['dp'=8,'tensor'=4] {'dp'}, dimensions={0}, use_global_device_ids=true | all-gather | bytes 663552 | tf_op jit(solution)/shard_map/all_gather | solution.py:88
  142.8 68.2 %gather_fusion = f32[16384,384]{1,0:T(8,128)} fusion(f32[384,128]{0,1:T(8,128)S(1)} %bitcast.583, s32[16384]{0:T(1024)} %broadcast_clamp_fusion), kind=kCustom, calls=%fused_computation | custom fusion | bytes 50397184 | tf_op jit(solution)/shard_map/jvp()/gather | solution.py:30
  335.9 43.1 %bitcast_add_fusion.7 = f32[1,8,128,384]{2,1,3,0:T(8,128)} fusion(f32[384,8,128]{2,1,0:T(8,128)S(1)} %fusion.55, f32[8,128,384]{1,0,2:T(8,128)S(1)} %copy-done.21, f32[128,128,384]{1,0,2:T(8,128)} %copy.201, pred[128,128]{1,0:T(8,128)(4,1)S(1)} %subtract_compare_fusion), kind=kOutput, calls=%fused_computation.305 | convolution fusion | flops 610664448 | bytes 29900800 | tf_op jit(solution)/shard_map/jvp(hts,absh->abth)/dot_general | solution.py:32
  379.0 40.6 %bitcast_add_fusion.5 = f32[1,8,128,384]{2,1,3,0:T(8,128)} fusion(f32[384,8,128]{2,1,0:T(8,128)S(1)} %fusion.53, f32[8,128,384]{1,0,2:T(8,128)S(1)} %copy.215, f32[128,128,384]{1,0,2:T(8,128)S(1)} %bitcast.585, pred[128,128]{1,0:T(8,128)(4,1)S(1)} %subtract_compare_fusion), kind=kOutput, calls=%fused_computation.303 | convolution fusion | flops 610664448 | bytes 29900800 | tf_op jit(solution)/shard_map/jvp(hts,absh->abth)/dot_general | solution.py:32
  488.2 63.0 %gather_fusion.1 = f32[16384,384]{1,0:T(8,128)} fusion(f32[384,128]{0,1:T(8,128)S(1)} %bitcast.582, s32[16384]{0:T(1024)S(1)} %copy-done.102), kind=kCustom, calls=%fused_computation.1 | custom fusion | bytes 50397184 | tf_op jit(solution)/shard_map/jvp()/gather | solution.py:30
  576.1 43.5 %bitcast_add_fusion.6 = f32[1,8,128,384]{2,1,3,0:T(8,128)} fusion(f32[384,8,128]{2,1,0:T(8,128)S(1)} %copy-done.74, f32[8,128,384]{1,0,2:T(8,128)S(1)} %copy.210, f32[128,128,384]{1,0,2:T(8,128)} %copy.209, pred[128,128]{1,0:T(8,128)(4,1)S(1)} %subtract_compare_fusion), kind=kOutput, calls=%fused_computation.304 | convolution fusion | flops 610664448 | bytes 29900800 | tf_op jit(solution)/shard_map/jvp(hts,absh->abth)/dot_general | solution.py:32
  685.4 42.9 %bitcast_add_fusion.4 = f32[1,8,128,384]{2,1,3,0:T(8,128)} fusion(f32[384,8,128]{2,1,0:T(8,128)S(1)} %fusion.37, f32[8,128,384]{1,0,2:T(8,128)S(1)} %copy.220, f32[128,128,384]{1,0,2:T(8,128)} %copy.209, pred[128,128]{1,0:T(8,128)(4,1)S(1)} %subtract_compare_fusion), kind=kOutput, calls=%fused_computation.302 | convolution fusion | flops 610664448 | bytes 29900800 | tf_op jit(solution)/shard_map/jvp(hts,absh->abth)/dot_general | solution.py:32
  808.2 65.5 %reduce-scatter.8.cloned.1.call-done = f32[1024,768]{1,0:T(8,128)} async-done(((f32[1024,3072]{1,0:T(8,128)}), f32[1024,768]{1,0:T(8,128)}) %reduce-scatter.8.cloned.1.call-update) | async-done | bytes 3145744 | tf_op jit(solution)/shard_map/reduce_scatter | solution.py:116
  873.7 99.7 %reduce-scatter.10.cloned.1.call-done = f32[1024,768]{1,0:T(8,128)} async-done(((f32[1024,3072]{1,0:T(8,128)}), f32[1024,768]{1,0:T(8,128)}) %reduce-scatter.10.cloned.1.call-update) | async-done | bytes 3145744 | tf_op jit(solution)/shard_map/reduce_scatter | solution.py:116
  1004.7 32.3 all-gather.15.cloned.1.call-done
  1322.1 42.6 %select_bitcast_fusion.3 = f32[128,128,384]{1,0,2:T(8,128)} fusion(pred[128,128]{1,0:T(8,128)(4,1)S(1)} %subtract_compare_fusion, f32[8,128,384]{1,0,2:T(8,128)S(1)} %copy-done.22, f32[1,8,128,384]{2,1,3,0:T(8,128)S(1)} %copy.225), kind=kOutput, calls=%fused_computation.57 | convolution fusion | flops 610271232 | bytes 28327936 | tf_op jit(solution)/shard_map/transpose(jvp(hts,absh->abth))/dot_general | solution.py:32
  1364.8 42.7 %select_bitcast_fusion.1 = f32[128,128,384]{1,0,2:T(8,128)} fusion(pred[128,128]{1,0:T(8,128)(4,1)S(1)} %subtract_compare_fusion, f32[8,128,384]{1,0,2:T(8,128)S(1)} %copy-done.19, f32[1,8,128,384]{2,1,3,0:T(8,128)S(1)} %copy-done.16), kind=kOutput, calls=%fused_computation.55 | convolution fusion | flops 610271232 | bytes 28327936 | tf_op jit(solution)/shard_map/transpose(jvp(hts,absh->abth))/dot_general | solution.py:32
  1407.5 42.9 %select_bitcast_fusion = f32[128,128,384]{1,0,2:T(8,128)} fusion(pred[128,128]{1,0:T(8,128)(4,1)S(1)} %subtract_compare_fusion, f32[8,128,384]{1,0,2:T(8,128)S(1)} %copy-done.25, f32[1,8,128,384]{2,1,3,0:T(8,128)S(1)} %copy-done.13), kind=kOutput, calls=%fused_computation.54 | convolution fusion | flops 610271232 | bytes 28327936 | tf_op jit(solution)/shard_map/transpose(jvp(hts,absh->abth))/dot_general | solution.py:32
  1450.4 42.6 %select_bitcast_fusion.2 = f32[128,128,384]{1,0,2:T(8,128)} fusion(pred[128,128]{1,0:T(8,128)(4,1)S(1)} %subtract_compare_fusion, f32[8,128,384]{1,0,2:T(8,128)S(1)} %copy-done.28, f32[1,8,128,384]{2,1,3,0:T(8,128)S(1)} %copy.230), kind=kOutput, calls=%fused_computation.56 | convolution fusion | flops 610271232 | bytes 28327936 | tf_op jit(solution)/shard_map/transpose(jvp(hts,absh->abth))/dot_general | solution.py:32
  1566.3 29.1 multiply_reduce_fusion.9
  1629.1 27.2 while.132
  1656.4 28.7 multiply_reduce_fusion.13
  1699.9 27.3 while.135
  1727.2 28.5 multiply_reduce_fusion.1
  1789.5 27.2 while.134
  1816.8 28.4 multiply_reduce_fusion.5
  1883.6 103.9 %scatter_custom_fusion = f32[384,128]{0,1:T(8,128)S(1)} fusion(s32[16384]{0:T(1024)} %maximum_bitcast_fusion, f32[16384,384]{1,0:T(8,128)} %bitcast.591, f32[]{:T(128)} %constant.222.clone.1), kind=kCustom, calls=%fused_computation.435 | custom fusion | flops 6291456 | bytes 197120 | tf_op jit(solution)/shard_map/transpose(jvp())/scatter-add | solution.py:30
  2013.1 103.9 %scatter_custom_fusion.2 = f32[384,128]{0,1:T(8,128)S(1)} fusion(s32[16384]{0:T(1024)} %maximum_bitcast_fusion, f32[16384,384]{1,0:T(8,128)} %bitcast.592, f32[]{:T(128)} %constant.222.clone.1), kind=kCustom, calls=%fused_computation.431 | custom fusion | flops 6291456 | bytes 197120 | tf_op jit(solution)/shard_map/transpose(jvp())/scatter-add | solution.py:30
  2142.6 103.9 %scatter_custom_fusion.3 = f32[384,128]{0,1:T(8,128)S(1)} fusion(s32[16384]{0:T(1024)} %maximum_bitcast_fusion, f32[16384,384]{1,0:T(8,128)} %bitcast.593, f32[]{:T(128)} %constant.222.clone.1), kind=kCustom, calls=%fused_computation.429 | custom fusion | flops 6291456 | bytes 197120 | tf_op jit(solution)/shard_map/transpose(jvp())/scatter-add | solution.py:30
  2272.0 104.1 %scatter_custom_fusion.1 = f32[384,128]{0,1:T(8,128)S(1)} fusion(s32[16384]{0:T(1024)} %maximum_bitcast_fusion, f32[16384,384]{1,0:T(8,128)} %bitcast.590, f32[]{:T(128)} %constant.222.clone.1), kind=kCustom, calls=%fused_computation.433 | custom fusion | flops 6291456 | bytes 197120 | tf_op jit(solution)/shard_map/transpose(jvp())/scatter-add | solution.py:30
  2469.8 77.8 %multiply_reduce_fusion.6 = (f32[384,64]{1,0:T(8,128)S(1)}, f32[384,64]{1,0:T(8,128)S(1)}, f32[384,64]{1,0:T(8,128)S(1)}, f32[384,64]{1,0:T(8,128)S(1)}, f32[384...) fusion(f32[128]{0:T(128)S(1)} %copy-done.174, ...), kind=kOutput, calls=%fused_computation.80 | convolution fusion | flops 440107008 | bytes 42467840 | tf_op jit(solution)/shard_map/transpose(jvp(hnt,bahn->abth))/dot_general | solution.py:43
  2631.6 219.4 %all-reduce.8.cloned.1.call-done = (f32[1024,768]{1,0:T(8,128)}, f32[1024,768]{1,0:T(8,128)}, f32[1024,768]{1,0:T(8,128)}, f32[1024,768]{1,0:T(8,128)}) async-done(((f32[1024,768]{1,0:T(8,128)}, f32[1024,768]{1,0:T(8,128)}, f32[1024,768]{1,0:T(8,128)}, f32[1024,768]{1,0:T(8,128)}), (f32[1024,768]{1,0:T(8,128)}, f32[1024,768]{1,0:T(8,128)}, f32[1024,768]{1,0:T(8,128)}, ...) | async-done | bytes 12582928 | tf_op jit(solution)/shard_map/psum | solution.py:120
  2863.9 37.7 %all-reduce = (f32[768]{0:T(1024)}, f32[768]{0:T(1024)}, f32[768]{0:T(1024)}, f32[384]{0:T(512)}, f32[768]{0:T(1024)}, /*index=5*/f32[768]{0:T(1024)}, f32[2,384]{1,0:T(2,128)}, f32[2,384]{1,0:T(2,128)}) all-reduce(f32[768]{0:T(1024)S(1)} %add.461, f32[768]{0:T(1024)S(1)} %add.462, ...), channel_id=1, replica_groups=mesh['dp'=8,'tensor'=4] {'dp'}, use_global_device_ids=true, to_apply=%region_32.33 | all-reduce | flops 5760 | bytes 46080 | tf_op jit(solution)/shard_map/psum | solution.py:211
  2925.2 72.9 %reduce-scatter.20.cloned.1.call-done = f32[768,96]{0,1:T(8,128)} async-done(((f32[768,768]{0,1:T(8,128)}), f32[768,96]{0,1:T(8,128)}) %reduce-scatter.20.cloned.1.call-update) | async-done | bytes 294928 | tf_op jit(solution)/shard_map/reduce_scatter | solution.py:208
  2998.1 68.1 %reduce-scatter.14.cloned.1.call-done = f32[96,384]{1,0:T(8,128)} async-done(((f32[768,384]{1,0:T(8,128)}), f32[96,384]{1,0:T(8,128)}) %reduce-scatter.14.cloned.1.call-update) | async-done | bytes 147472 | tf_op jit(solution)/shard_map/reduce_scatter | solution.py:205
  3066.2 98.7 %reduce-scatter.16.cloned.1.call-done = f32[384,384]{1,0:T(8,128)} async-done(((f32[384,3072]{1,0:T(8,128)}), f32[384,384]{1,0:T(8,128)}) %reduce-scatter.16.cloned.1.call-update) | async-done | bytes 589840 | tf_op jit(solution)/shard_map/reduce_scatter | solution.py:206
  3164.9 99.4 %reduce-scatter.18.cloned.1.call-done = f32[384,384]{1,0:T(8,128)} async-done(((f32[384,3072]{1,0:T(8,128)}), f32[384,384]{1,0:T(8,128)}) %reduce-scatter.18.cloned.1.call-update) | async-done | bytes 589840 | tf_op jit(solution)/shard_map/reduce_scatter | solution.py:207
  (849 shorter events, 1441.2 us)
Async XLA Ops:
  7.2 749.3 %all-gather.7.cloned.1.call-start = ((), (), s32[]{:S(2)}) async-start(), calls=%async_computation.7 | async-start | bytes 2654208 | tf_op jit(solution)/shard_map/all_gather | solution.py:89
  7.9 758.6 %all-gather.9.cloned.1.call-start = ((), (), s32[]{:S(2)}) async-start(), calls=%async_computation.8 | async-start | bytes 2654208 | tf_op jit(solution)/shard_map/all_gather | solution.py:90
  8.7 785.3 %all-gather.11.cloned.1.call-start = ((), (), s32[]{:S(2)}) async-start(), calls=%async_computation.10 | async-start | bytes 1327104 | tf_op jit(solution)/shard_map/all_gather | solution.py:87
  9.4 790.3 %all-gather.13.cloned.1.call-start = ((), (), s32[]{:S(2)}) async-start(), calls=%async_computation.11 | async-start | bytes 1327104 | tf_op jit(solution)/shard_map/all_gather | solution.py:91
  10.0 863.7 %reduce-scatter.8.cloned.1.call-start = ((), (), s32[]{:S(2)}) async-start(), calls=%async_computation.9 | async-start | bytes 15728640 | tf_op jit(solution)/shard_map/reduce_scatter | solution.py:116
  255.1 123.9 %copy-start.18 = (f32[8,128,384]{1,0,2:T(8,128)}, f32[8,128,384]{1,0,2:T(8,128)S(1)}, u32[]{:S(2)}) copy-start(f32[8,128,384]{1,0,2:T(8,128)S(1)} %copy.215) | copy-start | bytes 4718596
  316.8 62.2 %slice-start = ((s8[25165824]{0:T(1024)(128)(4,1)}), s8[4194304]{0:T(1024)(128)(4,1)S(1)}, s32[]{:S(2)}) async-start(s8[25165824]{0:T(1024)(128)(4,1)} %bitcast.584), calls=%async_computation.22 | async-start | bytes 8388608
  316.8 62.2 %slice-start.1 = ((s8[25165824]{0:T(1024)(128)(4,1)}), s8[4194304]{0:T(1024)(128)(4,1)S(1)}, s32[]{:S(2)}) async-start(s8[25165824]{0:T(1024)(128)(4,1)} %bitcast.584), calls=%async_computation.23 | async-start | bytes 8388608
  420.2 155.8 %copy-start.27 = (f32[8,128,384]{1,0,2:T(8,128)}, f32[8,128,384]{1,0,2:T(8,128)S(1)}, u32[]{:S(2)}) copy-start(f32[8,128,384]{1,0,2:T(8,128)S(1)} %copy.210) | copy-start | bytes 4718596
  623.3 62.1 %copy-start.24 = (f32[8,128,384]{1,0,2:T(8,128)}, f32[8,128,384]{1,0,2:T(8,128)S(1)}, u32[]{:S(2)}) copy-start(f32[8,128,384]{1,0,2:T(8,128)S(1)} %copy.220) | copy-start | bytes 4718596
  776.4 196.9 %reduce-scatter.10.cloned.1.call-start = ((), (), s32[]{:S(2)}) async-start(), calls=%async_computation.12 | async-start | bytes 15728640 | tf_op jit(solution)/shard_map/reduce_scatter | solution.py:116
  793.9 243.1 %all-gather.15.cloned.1.call-start = ((), (), s32[]{:S(2)}) async-start(), calls=%async_computation.13 | async-start | bytes 7864320 | tf_op jit(solution)/shard_map/all_gather | solution.py:150
  804.8 168.5 %copy-start.131 = (f32[1024]{0:T(1024)S(1)}, f32[1024]{0:T(1024)}, u32[]{:S(2)}) copy-start(f32[1024]{0:T(1024)} %copy-done.130) | copy-start | bytes 12292
  804.9 168.5 %copy-start.166 = (f32[768]{0:T(1024)S(1)}, f32[768]{0:T(1024)}, u32[]{:S(2)}) copy-start(f32[768]{0:T(1024)} %param.45) | copy-start | bytes 9220
  804.9 168.5 %copy-start.167 = (f32[768]{0:T(1024)S(1)}, f32[768]{0:T(1024)}, u32[]{:S(2)}) copy-start(f32[768]{0:T(1024)} %param.40) | copy-start | bytes 9220
  990.4 174.0 %all-gather.17.cloned.1.call-start = ((), (), s32[]{:S(2)}) async-start(), calls=%async_computation.14 | async-start | bytes 7864320 | tf_op jit(solution)/shard_map/all_gather | solution.py:150
  991.2 1636.8 %all-reduce.6.cloned.1.call-start = ((), (), s32[]{:S(2)}) async-start(), calls=%async_computation.20 | async-start | bytes 1572864 | tf_op jit(solution)/shard_map/psum | solution.py:211
  1091.5 50.4 %slice-start.6 = ((s8[25165824]{0:T(1024)(128)(4,1)}), s8[4194304]{0:T(1024)(128)(4,1)S(1)}, s32[]{:S(2)}) async-start(s8[25165824]{0:T(1024)(128)(4,1)} %bitcast.586), calls=%async_computation.28 | async-start | bytes 8388608
  2469.7 78.0 %copy-start.63 = (f32[384,64]{1,0:T(8,128)S(1)}, f32[384,64]{1,0:T(8,128)}, u32[]{:S(2)}) copy-start(f32[384,64]{1,0:T(8,128)} %copy-done.62) | copy-start | bytes 294916
  2469.7 78.0 %copy-start.85 = (f32[1,384,64]{2,1,0:T(8,128)S(1)}, f32[1,384,64]{2,1,0:T(8,128)}, u32[]{:S(2)}) copy-start(f32[1,384,64]{2,1,0:T(8,128)} %copy.297) | copy-start | bytes 294916
  2469.7 78.0 %copy-start.101 = (f32[384,64]{1,0:T(8,128)S(1)}, f32[384,64]{1,0:T(8,128)}, u32[]{:S(2)}) copy-start(f32[384,64]{1,0:T(8,128)} %copy-done.96) | copy-start | bytes 294916
  2469.7 78.0 %copy-start.104 = (f32[384,64]{1,0:T(8,128)S(1)}, f32[384,64]{1,0:T(8,128)}, u32[]{:S(2)}) copy-start(f32[384,64]{1,0:T(8,128)} %multiply_reduce_fusion.13) | copy-start | bytes 294916
  2469.8 78.0 %copy-start.106 = (f32[384,64]{1,0:T(8,128)S(1)}, f32[384,64]{1,0:T(8,128)}, u32[]{:S(2)}) copy-start(f32[384,64]{1,0:T(8,128)} %multiply_reduce_fusion.5) | copy-start | bytes 294916
  2469.8 78.0 %copy-start.108 = (f32[384,1,64]{2,1,0:T(1,128)S(1)}, f32[384,1,64]{2,1,0:T(1,128)}, u32[]{:S(2)}) copy-start(f32[384,1,64]{2,1,0:T(1,128)} %fusion.61) | copy-start | bytes 294916
  2469.8 78.0 %copy-start.109 = (f32[384,1,64]{2,1,0:T(1,128)S(1)}, f32[384,1,64]{2,1,0:T(1,128)}, u32[]{:S(2)}) copy-start(f32[384,1,64]{2,1,0:T(1,128)} %fusion.62) | copy-start | bytes 294916
  2469.8 78.0 %copy-start.149 = (f32[384]{0:T(512)S(1)}, f32[384]{0:T(512)}, u32[]{:S(2)}) copy-start(f32[384]{0:T(512)} %get-tuple-element.1073) | copy-start | bytes 4612
  2552.6 298.4 %all-reduce.8.cloned.1.call-start = ((), (), s32[]{:S(2)}) async-start(), calls=%async_computation.21 | async-start | bytes 25165824 | tf_op jit(solution)/shard_map/psum | solution.py:120
  2557.2 367.9 %reduce-scatter.12.cloned.1.call-start = ((), (), s32[]{:S(2)}) async-start(), calls=%async_computation.15 | async-start | bytes 2654208 | tf_op jit(solution)/shard_map/reduce_scatter | solution.py:204
  2564.2 433.8 %reduce-scatter.20.cloned.1.call-start = ((), (), s32[]{:S(2)}) async-start(), calls=%async_computation.19 | async-start | bytes 2654208 | tf_op jit(solution)/shard_map/reduce_scatter | solution.py:208
  2571.3 494.8 %reduce-scatter.14.cloned.1.call-start = ((), (), s32[]{:S(2)}) async-start(), calls=%async_computation.16 | async-start | bytes 1327104 | tf_op jit(solution)/shard_map/reduce_scatter | solution.py:205
  2576.5 588.4 %reduce-scatter.16.cloned.1.call-start = ((), (), s32[]{:S(2)}) async-start(), calls=%async_computation.17 | async-start | bytes 5308416 | tf_op jit(solution)/shard_map/reduce_scatter | solution.py:206
  2589.3 675.0 %reduce-scatter.18.cloned.1.call-start = ((), (), s32[]{:S(2)}) async-start(), calls=%async_computation.18 | async-start | bytes 5308416 | tf_op jit(solution)/shard_map/reduce_scatter | solution.py:207
  (180 other events, 3065.6 us)
Sparse Core Ops, SparseCore 0:
  10.1 61.9 all-gather.6
  74.1 52.4 all-gather.8
  128.8 39.2 all-gather.10
  170.1 39.8 all-gather.12
  776.5 97.1 reduce-scatter.7
  876.2 97.1 reduce-scatter.9
  990.5 46.3 all-gather.14
  1038.5 46.3 all-gather.16
  2552.7 75.2 all-reduce.5
  2631.1 219.8 all-reduce.7
  2855.1 70.0 reduce-scatter.11
  2929.1 68.9 reduce-scatter.19
  3002.0 64.0 reduce-scatter.13
  3070.2 94.5 reduce-scatter.15
  3168.9 95.2 reduce-scatter.17
where the time goes:
time: 3290 us; the launch traced here: 3270 us
  matrix products  1290 us (39%)
  waiting for transfers between devices  785 us (24%)
  other arithmetic  565 us (17%)
  local copies, waits for them, and re-layouts  539 us (16%)
  blocking collectives  73 us (2%)
    dot_general x12, matrix products, causal_scan(): inside = jnp.einsum('hts,absh->abth', toeplitz, pieces, precision=PRECISE)  438 us
    scatter-add x4, other arithmetic, causal_scan(): kernel[:, jnp.maximum(lag_index, 0)]  416 us
    dot_general x12, matrix products, causal_scan(): outside = jnp.einsum('hnt,bahn->abth', opening, before, precision=PRECISE)  326 us
    dot_general x12, matrix products, causal_scan(): summary = jnp.einsum('hns,absh->abhn', closing, pieces, precision=PRECISE)  253 us
    psum x1, waiting for transfers between devices, shards(): lax.psum(jnp.dot(hidden, output_full, preferred_element_type=jnp.float32)...  219 us
    gather x4, local copies, waits for them, and re-layouts, causal_scan(): kernel[:, jnp.maximum(lag_index, 0)]  181 us
    reduce_scatter x2, waiting for transfers between devices, shards(): lax.psum_scatter(mixed_part, 'tensor', scatter_dimension=1, tiled=True)  165 us
    dot_general x6, matrix products, causal_scan(): kernel = jnp.einsum('hn,hnk->hk', weights, powers, precision=PRECISE)  107 us
  transfers between devices with their start and end apart: 15, of which 10 were waited for; matrix products, arithmetic and copies ran while one was open for 30% of the time, Pallas kernels for 0%

commit v1 on v0

v1 whole, which is shorter than its diff:
```python
import math

import jax
import jax.numpy as jnp
from jax import lax
from jax.experimental import pallas as pl
from jax.experimental.pallas import tpu as pltpu
from jax.sharding import PartitionSpec as P

EPSILON = 1e-05
LANES = 128
INNER = 32
BF = jnp.bfloat16
F32 = jnp.float32
GELU_C = math.sqrt(2.0 / math.pi)
GELU_A = 0.044715


def gelu_pair(x):
    square = x * x
    bend = jnp.tanh(GELU_C * x * (1.0 + GELU_A * square))
    half = 0.5 * (1.0 + bend)
    slope = half + 0.5 * x * (1.0 - bend * bend) * (GELU_C * (1.0 + 3.0 * GELU_A * square))
    return x * half, slope


def dot_nt(a, b):
    return lax.dot_general(a, b, (((1,), (1,)), ((), ())), preferred_element_type=F32)


def dot_tn(a, b):
    return lax.dot_general(a, b, (((0,), (0,)), ((), ())), preferred_element_type=F32)


def dot_nn(a, b):
    return jnp.dot(a, b, preferred_element_type=F32)


def fill_powers(rate_ref, one_ref, many_ref, scale):
    states = rate_ref.shape[0]
    offset = lax.broadcasted_iota(jnp.int32, (INNER, LANES), 0).astype(F32)

    def body(n, _):
        row = rate_ref[pl.ds(n, 1), :]
        one_ref[n] = jnp.exp(-(row * offset))
        wide = jnp.exp(-(row * (offset * float(INNER))))
        if scale is not None:
            wide = wide * scale[pl.ds(n, 1), :]
        many_ref[n] = wide
        return 0

    lax.fori_loop(0, states, body, 0)


def impulse_kernel(delta_ref, rate_ref, readout_ref, out_ref, a_ref, w_ref, one_ref, many_ref):
    states = rate_ref.shape[1]
    length = out_ref.shape[0]
    step = jnp.exp(delta_ref[0])
    a_ref[...] = step * rate_ref[0]
    w_ref[...] = step * readout_ref[0]
    fill_powers(a_ref, one_ref, many_ref, w_ref)
    group = 8
    for start in range(0, length // INNER, group):

        def body(n, sums):
            base = one_ref[n]
            return tuple(
                total + many_ref[n, start + j : start + j + 1, :] * base
                for j, total in enumerate(sums)
            )

        sums = lax.fori_loop(
            0, states, body, tuple(jnp.zeros((INNER, LANES), F32) for _ in range(group))
        )
        for j, total in enumerate(sums):
            at = (start + j) * INNER
            out_ref[at : at + INNER, :] = total


def impulse(delta, rate, readout, length):
    dirs, states, channels = rate.shape
    lanes = channels // LANES
    spec = pl.BlockSpec((1, states, LANES), lambda c, j: (c, 0, j))
    return pl.pallas_call(
        impulse_kernel,
        name="impulse",
        grid=(dirs, lanes),
        in_specs=[pl.BlockSpec((1, 1, LANES), lambda c, j: (c, 0, j)), spec, spec],
        out_specs=pl.BlockSpec((length, LANES), lambda c, j: (0, c * lanes + j)),
        out_shape=jax.ShapeDtypeStruct((length, dirs * channels), F32),
        scratch_shapes=[
            pltpu.VMEM((states, LANES), F32),
            pltpu.VMEM((states, LANES), F32),
            pltpu.VMEM((states, INNER, LANES), F32),
            pltpu.VMEM((states, length // INNER, LANES), F32),
        ],
    )(delta, rate, readout)


def state_grad_kernel(
    delta_ref, rate_ref, readout_ref, grad_ref, gdelta_ref, grate_ref, greadout_ref, a_ref, one_ref, many_ref, g_ref, m_ref
):
    states = rate_ref.shape[1]
    length = grad_ref.shape[0]
    step = jnp.exp(delta_ref[0])
    a_ref[...] = step * rate_ref[0]
    fill_powers(a_ref, one_ref, many_ref, None)
    offset = lax.broadcasted_iota(jnp.int32, (INNER, LANES), 0).astype(F32)
    group = 4
    zero = jnp.zeros((INNER, LANES), F32)

    def body(i, _):
        sums = [zero] * group
        moments = [zero] * group
        for k in range(length // INNER - 1, -1, -1):
            block = grad_ref[k * INNER : (k + 1) * INNER, :]
            for j in range(group):
                sums[j] = sums[j] + many_ref[i * group + j, k : k + 1, :] * block
                if k > 0:
                    moments[j] = moments[j] + sums[j]
        for j in range(group):
            n = i * group + j
            base = one_ref[n]
            g_ref[pl.ds(n, 1), :] = jnp.sum(base * sums[j], axis=0, keepdims=True)
            m_ref[pl.ds(n, 1), :] = jnp.sum(
                base * (offset * sums[j] + float(INNER) * moments[j]), axis=0, keepdims=True
            )
        return 0

    lax.fori_loop(0, states // group, body, 0)
    rate = rate_ref[0]
    readout = readout_ref[0]
    grad_w = g_ref[...]
    grad_a = -(step * readout) * m_ref[...]
    greadout_ref[0] = step * grad_w
    grate_ref[0] = step * grad_a
    gdelta_ref[0] = step * jnp.sum(readout * grad_w + rate * grad_a, axis=0, keepdims=True)


def state_grad(delta, rate, readout, grad):
    dirs, states, channels = rate.shape
    length = grad.shape[0]
    lanes = channels // LANES
    spec = pl.BlockSpec((1, states, LANES), lambda c, j: (c, 0, j))
    row = pl.BlockSpec((1, 1, LANES), lambda c, j: (c, 0, j))
    return pl.pallas_call(
        state_grad_kernel,
        name="state_grad",
        grid=(dirs, lanes),
        in_specs=[row, spec, spec, pl.BlockSpec((length, LANES), lambda c, j: (0, c * lanes + j))],
        out_specs=[row, spec, spec],
        out_shape=[
            jax.ShapeDtypeStruct((dirs, 1, channels), F32),
            jax.ShapeDtypeStruct((dirs, states, channels), F32),
            jax.ShapeDtypeStruct((dirs, states, channels), F32),
        ],
        scratch_shapes=[
            pltpu.VMEM((states, LANES), F32),
            pltpu.VMEM((states, INNER, LANES), F32),
            pltpu.VMEM((states, length // INNER, LANES), F32),
            pltpu.VMEM((states, LANES), F32),
            pltpu.VMEM((states, LANES), F32),
        ],
    )(delta, rate, readout, grad)


def fourier(length):
    period = 4 * length
    odd = 2 * jnp.arange(length, dtype=jnp.int32)[:, None] + 1
    unit = 2.0 * math.pi / period

    def table(times):
        angle = ((odd * times[None, :]) % period).astype(F32) * unit
        return jnp.cos(angle), jnp.sin(angle)

    fine_cos, fine_sin = table(jnp.arange(LANES, dtype=jnp.int32))
    wide_cos, wide_sin = table(jnp.arange(length // LANES, dtype=jnp.int32) * LANES)
    cos_parts = []
    sin_parts = []
    for j in range(length // LANES):
        c, s = wide_cos[:, j : j + 1], wide_sin[:, j : j + 1]
        cos_parts.append(c * fine_cos - s * fine_sin)
        sin_parts.append(s * fine_cos + c * fine_sin)
    whole = jnp.concatenate(
        [jnp.concatenate(cos_parts, axis=1), jnp.concatenate(sin_parts, axis=1)], axis=0
    )
    return whole.astype(BF)


def make_shards(tensor_size):
    core_swap = [(i, i ^ 1) for i in range(tensor_size)]
    far_swap = [(i, i ^ 2) for i in range(tensor_size)]

    def near(v):
        return lax.ppermute(v, "tensor", core_swap)

    def far(v):
        return lax.ppermute(v, "tensor", far_swap)

    def shards(
        inputs,
        cotangent,
        lengths,
        norm_gain,
        norm_bias,
        value_weight,
        value_bias,
        feed_weight,
        feed_bias,
        mix_forward,
        mix_backward,
        mix_bias,
        out_weight,
        out_bias,
        state_delta,
        state_rate,
        state_readout,
        state_skip,
    ):
        slots, length, width = inputs.shape
        channels = feed_weight.shape[1]
        hidden_width = value_weight.shape[1]
        me = lax.axis_index("tensor")
        core = me % 2
        half = length // 2

        first_own = jnp.concatenate([feed_weight, value_weight], axis=1)
        first_all = lax.all_gather(first_own, "dp", axis=0, tiled=True)
        mix_own = jnp.concatenate([mix_forward.T, mix_backward.T], axis=1)
        mix_all = lax.all_gather(mix_own, "dp", axis=0, tiled=True)
        out_all = lax.all_gather(out_weight.T, "dp", axis=0, tiled=True)
        feed_full = first_all[:, :channels]
        value_full = first_all[:, channels:]
        mix_blocks = mix_all.reshape(tensor_size, hidden_width, 2 * channels)
        mix_of = [
            lax.dynamic_index_in_dim(mix_blocks, me ^ j, axis=0, keepdims=False)
            for j in range(tensor_size)
        ]
        mix_send = jnp.concatenate([mix_of[1], mix_of[3]], axis=0)

        delta = state_delta[:, None, :]
        rate = jnp.swapaxes(state_rate, 1, 2)
        readout = jnp.swapaxes(state_readout, 1, 2)
        wave = fourier(length)
        response = impulse(delta, rate, readout, length)
        response_f = dot_nn(wave, response.astype(BF))
        k0c, k1c = response_f[:length, :channels], response_f[:length, channels:]
        k0s, k1s = response_f[length:, :channels], response_f[length:, channels:]
        scale = 1.0 / length

        time_at = jnp.arange(length)[:, None]
        skip_row = state_skip.reshape(1, 2 * channels)

        saved = []
        layer_rows = []
        grad_mix = [None] * tensor_size
        for slot in range(slots):
            rows = inputs[slot].astype(F32)
            live = (time_at < lengths[slot]).astype(F32)
            center = rows - jnp.mean(rows, axis=-1, keepdims=True)
            spread = jnp.mean(center * center, axis=-1, keepdims=True)
            normed = (center * lax.rsqrt(spread + EPSILON) * norm_gain + norm_bias).astype(BF)
            feed_pre = dot_nn(normed, feed_full) + feed_bias
            signal = gelu_pair(feed_pre)[0] * live
            signal_low = signal.astype(BF)
            signal_f = dot_nn(wave, signal_low)
            uc, us = signal_f[:length], signal_f[length:]
            product = jnp.concatenate(
                [
                    jnp.concatenate([uc * k0c - us * k0s, uc * k1c + us * k1s], axis=1),
                    jnp.concatenate([uc * k0s + us * k0c, us * k1c - uc * k1s], axis=1),
                ],
                axis=0,
            )
            scanned = dot_tn(wave, (product * scale).astype(BF))
            both = (scanned + skip_row * jnp.concatenate([signal, signal], axis=1)).astype(BF)

            sent = dot_nt(both, mix_send).astype(BF)
            received = near(sent)
            passed = (dot_nt(both, mix_of[2]) + received[:, hidden_width:].astype(F32)).astype(BF)
            own = dot_nt(both, mix_of[0]) + received[:, :hidden_width].astype(F32)
            mixed = own + far(passed).astype(F32) + mix_bias

            value_pre = dot_nn(normed, value_full) + value_bias
            upstream_low = (cotangent[slot].astype(F32) * live).astype(BF)
            grad_hidden = dot_nn(upstream_low, out_all)
            saved.append((normed, feed_pre, live, signal, uc, us, both, mixed, value_pre, upstream_low, grad_hidden))

        grads = []
        for slot in range(slots):
            normed, feed_pre, live, signal, uc, us, both, mixed, value_pre, upstream_low, grad_hidden = saved[slot]
            value_act, value_slope = gelu_pair(value_pre)
            gate_act, gate_slope = gelu_pair(mixed)
            hidden = (gate_act * value_act).astype(BF)
            grad_gate = (gate_slope * grad_hidden * value_act).astype(BF)
            grad_value = (value_slope * grad_hidden * gate_act).astype(BF)
            pieces = [grad_gate, near(grad_gate), far(grad_gate)]
            pieces.append(near(pieces[2]))
            grads.append((hidden, grad_value, pieces))

        grad_value_w = None
        grad_out_w = None
        for slot in range(slots):
            normed, feed_pre, live, signal, uc, us, both, mixed, value_pre, upstream_low, grad_hidden = saved[slot]
            hidden, grad_value, pieces = grads[slot]
            branch = dot_nt(hidden, out_all)
            give = lax.dynamic_slice_in_dim(branch, (1 - core) * half, half, 0).astype(BF)
            keep = lax.dynamic_slice_in_dim(branch, core * half, half, 0)
            pair = lax.optimization_barrier((keep + near(give).astype(F32)).astype(BF))
            other = far(pair)
            rows_half = lax.dynamic_slice_in_dim(inputs[slot], core * half, half, 0).astype(F32)
            live_half = lax.dynamic_slice_in_dim(live, core * half, half, 0)
            mine = (
                live_half * (rows_half + (pair.astype(F32) + other.astype(F32)) + out_bias)
            ).astype(BF)
            theirs = near(mine)
            layer_rows.append(
                jnp.concatenate(
                    [jnp.where(core == 0, mine, theirs), jnp.where(core == 0, theirs, mine)], axis=0
                )
            )
            step_value = dot_tn(normed, grad_value)
            step_out = dot_tn(upstream_low, hidden)
            grad_value_w = step_value if slot == 0 else grad_value_w + step_value
            grad_out_w = step_out if slot == 0 else grad_out_w + step_out
        early = lax.psum_scatter(
            jnp.concatenate([grad_value_w.astype(BF), grad_out_w.astype(BF)], axis=1),
            "dp",
            scatter_dimension=0,
            tiled=True,
        ).astype(F32)

        input_rows = []
        grad_k = None
        grad_feed_w = None
        small = None
        for slot in range(slots):
            normed, feed_pre, live, signal, uc, us, both, mixed, value_pre, upstream_low, grad_hidden = saved[slot]
            hidden, grad_value, pieces = grads[slot]
            grad_both = dot_nn(pieces[0], mix_of[0])
            for j in (1, 2, 3):
                grad_both = grad_both + dot_nn(pieces[j], mix_of[j])
            for j in range(tensor_size):
                step = dot_tn(pieces[j], both)
                grad_mix[j] = step if slot == 0 else grad_mix[j] + step
            grad_f = dot_nn(wave, grad_both.astype(BF))
            ac, bc = grad_f[:length, :channels], grad_f[:length, channels:]
            as_, bs = grad_f[length:, :channels], grad_f[length:, channels:]
            back = jnp.concatenate(
                [
                    ac * k0c + as_ * k0s + bc * k1c - bs * k1s,
                    as_ * k0c - ac * k0s + bc * k1s + bs * k1c,
                ],
                axis=0,
            )
            grad_signal = dot_tn(wave, (back * scale).astype(BF))
            grad_signal = (
                grad_signal
                + state_skip[0] * grad_both[:, :channels]
                + state_skip[1] * grad_both[:, channels:]
            )
            lag = jnp.concatenate(
                [
                    jnp.concatenate([ac * uc + as_ * us, uc * bc + us * bs], axis=1),
                    jnp.concatenate([as_ * uc - ac * us, us * bc - uc * bs], axis=1),
                ],
                axis=0,
            )
            grad_k = lag if slot == 0 else grad_k + lag
            grad_skip = jnp.sum(grad_both * jnp.concatenate([signal, signal], axis=1), axis=0)
            grad_feed = (gelu_pair(feed_pre)[1] * live * grad_signal).astype(BF)
            features = dot_nt(grad_value, value_full) + dot_nt(grad_feed, feed_full)
            step_feed = dot_tn(normed, grad_feed)
            grad_feed_w = step_feed if slot == 0 else grad_feed_w + step_feed

            give = lax.dynamic_slice_in_dim(features, (1 - core) * half, half, 0).astype(BF)
            keep = lax.dynamic_slice_in_dim(features, core * half, half, 0)
            pair = lax.optimization_barrier((keep + near(give).astype(F32)).astype(BF))
            total = pair.astype(F32) + far(pair).astype(F32)
            rows = lax.dynamic_slice_in_dim(inputs[slot], core * half, half, 0).astype(F32)
            up_half = lax.dynamic_slice_in_dim(upstream_low, core * half, half, 0).astype(F32)
            center = rows - jnp.mean(rows, axis=-1, keepdims=True)
            spread = jnp.mean(center * center, axis=-1, keepdims=True)
            inverse = lax.rsqrt(spread + EPSILON)
            unit = center * inverse
            weighted = total * norm_gain
            mine = (
                up_half
                + (
                    weighted
                    - jnp.mean(weighted, axis=-1, keepdims=True)
                    - unit * jnp.mean(weighted * unit, axis=-1, keepdims=True)
                )
                * inverse
            ).astype(BF)
            theirs = near(mine)
            input_rows.append(
                jnp.concatenate(
                    [jnp.where(core == 0, mine, theirs), jnp.where(core == 0, theirs, mine)], axis=0
                )
            )
            now = (
                jnp.sum(total * unit, axis=0),
                jnp.sum(total, axis=0),
                jnp.sum(grad_value.astype(F32), axis=0),
                jnp.sum(grad_feed.astype(F32), axis=0),
                jnp.sum(pieces[0].astype(F32), axis=0),
                jnp.sum(upstream_low.astype(F32), axis=0),
                grad_skip,
            )
            small = now if slot == 0 else tuple(a + b for a, b in zip(small, now))

        mix_stack = jnp.stack([g.astype(BF) for g in grad_mix], axis=0)
        mix_natural = jnp.concatenate(
            [lax.dynamic_index_in_dim(mix_stack, me ^ b, axis=0, keepdims=False) for b in range(tensor_size)],
            axis=0,
        )
        mix_sum = lax.psum_scatter(mix_natural, "dp", scatter_dimension=0, tiled=True).astype(F32)
        feed_sum = lax.psum_scatter(
            grad_feed_w.astype(BF), "dp", scatter_dimension=0, tiled=True
        ).astype(F32)

        grad_response = dot_tn(wave, (grad_k * scale).astype(BF))
        grad_delta, grad_rate, grad_readout = state_grad(delta, rate, readout, grad_response)

        flat = jnp.concatenate([v.reshape(-1) for v in small] + [grad_delta.reshape(-1)])
        sums = lax.psum(flat, "dp")
        state_sums = lax.psum(jnp.concatenate([grad_rate, grad_readout], axis=0), "dp")
        at = 0
        parts = []
        for v in small + (grad_delta,):
            parts.append(sums[at : at + v.size])
            at += v.size
        norm_sums = jnp.stack([parts[0], parts[1]])
        norm_sums = norm_sums + near(norm_sums)
        state_sums = jnp.swapaxes(state_sums, 1, 2)

        return (
            jnp.stack(layer_rows),
            jnp.stack(input_rows),
            norm_sums[0],
            norm_sums[1],
            early[:, :hidden_width],
            parts[2],
            feed_sum,
            parts[3],
            mix_sum[:, :channels].T,
            mix_sum[:, channels:].T,
            parts[4],
            early[:, hidden_width:].T,
            parts[5],
            parts[7].reshape(2, channels),
            state_sums[:2],
            state_sums[2:],
            parts[6].reshape(2, channels),
        )

    return shards


def solution(mesh):
    placed = (
        P("dp", None, None),
        P("dp", None, None),
        P("dp"),
        P(),
        P(),
        P("dp", "tensor"),
        P("tensor"),
        P("dp", "tensor"),
        P("tensor"),
        P("tensor", "dp"),
        P("tensor", "dp"),
        P("tensor"),
        P("tensor", "dp"),
        P(),
        P(None, "tensor"),
        P(None, "tensor", None),
        P(None, "tensor", None),
        P(None, "tensor"),
    )
    return jax.shard_map(
        make_shards(mesh.shape["tensor"]),
        mesh=mesh,
        in_specs=placed,
        out_specs=(
            P("dp", None, None),
            P("dp", None, None),
            P(),
            P(),
            P("dp", "tensor"),
            P("tensor"),
            P("dp", "tensor"),
            P("tensor"),
            P("tensor", "dp"),
            P("tensor", "dp"),
            P("tensor"),
            P("tensor", "dp"),
            P(),
            P(None, "tensor"),
            P(None, "tensor", None),
            P(None, "tensor", None),
            P(None, "tensor"),
        ),
        check_vma=False,
    )
```

time: 3290 us -> 781 us (0.24)
  matrix products: 1290 us -> 165 us
  waiting for transfers between devices: 785 us -> 276 us
  local copies, waits for them, and re-layouts: 539 us -> 56.9 us
  other arithmetic: 565 us -> 133 us
  Pallas kernels: 0 us -> 73.1 us
  blocking collectives: 73 us -> 37.1 us
    dot_general x72 -> x50, matrix products: 1290 us -> 165 us  [the longest x19 70.8 us: dot_tn(): lax.dot_general(a, b, (((0,), (0,)), ((), ())), preferred_element_type=F32)]
    reduce_scatter x7 -> x2, waiting for transfers between devices: 517 us -> 84.7 us  [the longest x1 62.5 us: shards(): lax.psum_scatter(grad_feed_w.astype(BF), 'dp', scatter_dimension=0, tiled...]
    scatter-add x4 -> x0, other arithmetic: 416 us -> none  [causal_scan(): kernel[:, jnp.maximum(lag_index, 0)]]
    psum x2 -> x1, waiting for transfers between devices: 232 us -> 0.01 us  [shards(): lax.psum(jnp.concatenate([grad_rate, grad_readout], axis=0), 'dp')]
    gather x4 -> x0, local copies, waits for them, and re-layouts: 181 us -> none  [causal_scan(): kernel[:, jnp.maximum(lag_index, 0)]]
    another operation x26 -> x2, local copies, waits for them, and re-layouts: 109 us -> 0.01 us  [shards(): norm_sums = jnp.stack([parts[0], parts[1]])]
    ppermute x0 -> x23, waiting for transfers between devices: none -> 104 us  [the longest x8 104 us: far(): return lax.ppermute(v, 'tensor', far_swap)]
    dynamic_slice x64 -> x0, local copies, waits for them, and re-layouts: 98.9 us -> none  [causal_scan(): _, before = lax.scan(advance, initial, jnp.moveaxis(summary, 1, 0))]
  transfers between devices with their start and end apart: 15 -> 30, of which waited for: 10 -> 8; matrix products, arithmetic and copies ran while one was open for 30% -> 42% of each run, Pallas kernels for 0% -> 9%
where the time goes in v1:
time: 781 us; the launch traced here: 770 us
  waiting for transfers between devices  276 us (35%)
  matrix products  165 us (21%)
  other arithmetic  133 us (17%)
  Pallas kernels  73.1 us (9%)
  local copies, waits for them, and re-layouts  56.9 us (7%)
  blocking collectives  37.1 us (5%)
  between operations  16.1 us (2%)
  starting transfers between devices  13.4 us (2%)
    ppermute x8, waiting for transfers between devices, far(): return lax.ppermute(v, 'tensor', far_swap)  104 us
    unnamed x8, waiting for transfers between devices  71.3 us
    dot_general x19, matrix products, dot_tn(): lax.dot_general(a, b, (((0,), (0,)), ((), ())), preferred_element_type=F32)  70.8 us
    dot_general x19, matrix products, dot_nn(): return jnp.dot(a, b, preferred_element_type=F32)  62.8 us
    reduce_scatter x1, waiting for transfers between devices, shards(): lax.psum_scatter(grad_feed_w.astype(BF), 'dp', scatter_dimension=0, tiled...  62.5 us
    pallas_call x1, Pallas kernels, impulse(): pl.pallas_call(impulse_kernel, name='impulse', grid=(dirs, lanes), in_spe...  38.5 us
    psum x1, blocking collectives, shards(): sums = lax.psum(flat, 'dp')  37.1 us
    pallas_call x1, Pallas kernels, state_grad(): pl.pallas_call(state_grad_kernel, name='state_grad', grid=(dirs, lanes),...  34.6 us
  transfers between devices with their start and end apart: 30, of which 8 were waited for; matrix products, arithmetic and copies ran while one was open for 42% of the time, Pallas kernels for 9%

profile of v1, /device:TPU:0, one launch (start us, length us, event | category | flops | bytes accessed | tf_op | source)
XLA Modules:
  0.0 770.1 jit_solution(877692873195355652)
XLA Ops:
  21.7 38.5 %impulse.1 = f32[1024,768]{1,0:T(8,128)} custom-call(f32[2,1,384]{2,1,0:T(1,128)} %broadcast_in_dim.2.delta_ref, f32[2,64,384]{2,1,0:T(8,128)} %bitcast.278, f32[2,64,384]{2,1,0:T(8,128)} %bitcast.280), custom_call_target="tpu_custom_call" | custom-call | tf_op jit(solution)/shard_map/impulse/pallas_call | solution.py:84
  83.6 8.4 %fusion.96 = f32[2048,768]{0,1:T(8,128)} fusion(f32[1024,768]{1,0:T(8,128)S(1)} %copy-done.24, bf16[1024,1024]{1,0:T(8,128)(2,1)} %get-tuple-element.176, bf16[1024,1024]{1,0:T(8,128)(2,1)} %get-tuple-element.175), kind=kOutput, calls=%fused_computation.194 | convolution fusion | flops 3230400512 | bytes 13631488 | tf_op jit(solution)/shard_map/dot_general | solution.py:36
  92.1 4.3 multiply_multiply_fusion
  98.3 4.6 multiply_multiply_fusion.1
  110.9 8.8 %fusion.25 = bf16[1024,768]{1,0:T(8,128)(2,1)} fusion(f32[1024,384]{1,0:T(8,128)S(1)} %get-tuple-element.205, f32[768]{0:T(1024)S(1)} %mul.1449, f32[1024,384]{0,1:T(8,128)} %get-tuple-element.118, f32[1024,384]{0,1:T(8,128)} %get-tuple-element.119, f32[1024,384]{0,1:T(8,128)} %get-tuple-element.117, f32[1024,384]{0,1:T(8,128)} %get-tuple-element.116, ...), kind=kOutput, calls=%fused_computation.36 | convolution fusion | flops 3240624128 | bytes 13634560 | tf_op jit(solution)/shard_map/dot_general | solution.py:32
  119.7 6.3 fusion.30
  126.0 15.7 %all-gather.6.cloned.1.call-done = bf16[3072,768]{0,1:T(8,128)(2,1)} async-done(((bf16[384,768]{0,1:T(8,128)(2,1)}), bf16[3072,768]{0,1:T(8,128)(2,1)}) %all-gather.6.cloned.1.call-update) | async-done | bytes 4718608 | tf_op jit(solution)/shard_map/all_gather | solution.py:230
  141.7 19.7 %copy.42 = bf16[3072,768]{1,0:T(8,128)(2,1)} copy(bf16[3072,768]{0,1:T(8,128)(2,1)} %all-gather.6.cloned.1.call-done) | data formatting | bytes 9437184 | tf_op jit(solution)/shard_map/all_gather | solution.py:230
  163.5 4.9 convolution_convert_fusion.1
  168.4 4.9 convolution_convert_fusion
  184.7 4.1 convert_reduce_fusion.3
  209.8 24.4 %collective-permute-done.1 = bf16[1024,768]{1,0:T(8,128)(2,1)S(1)} collective-permute-done((bf16[1024,768]{1,0:T(8,128)(2,1)S(1)}, bf16[1024,768]{1,0:T(8,128)(2,1)S(1)}, u32[]{:S(2)}, u32[]{:S(2)}) %collective-permute-start.1) | collective-permute-done | bytes 1572896 | tf_op jit(solution)/shard_map/ppermute | solution.py:198
  235.3 31.7 %collective-permute-done.6 = bf16[1024,768]{1,0:T(8,128)(2,1)} collective-permute-done((bf16[1024,768]{1,0:T(8,128)(2,1)S(1)}, bf16[1024,768]{1,0:T(8,128)(2,1)}, u32[]{:S(2)}, u32[]{:S(2)}) %collective-permute-start.6) | collective-permute-done | bytes 1572896 | tf_op jit(solution)/shard_map/ppermute | solution.py:198
  267.1 10.5 %convert_reduce_fusion.5 = (f32[768]{0:T(1024)}, bf16[1024,768]{1,0:T(8,128)(2,1)S(1)}, f32[1024,768]{1,0:T(8,128)S(1)}, f32[768]{0:T(1024)}, bf16[1024,768]{1,0:T(8,128)(2,1)}, /*index=5*/f32[1024,768]{1,0:T(8,128)S(1)}) fusion(f32[1024,768]{1,0:T(8,128)S(1)} %fusion.145, f32[768]{0:T(1024)S(1)} %copy-done.76, f32[1024,768]{1,0:T(8,128)S(1)} %fusion.233, ...), kind=kLoop, calls=%fused_computation.57 | loop fusion | flops 55048704 | bytes 34615296 | tf_op jit(solution)/shard_map/reduce_sum | solution.py:407
  279.8 8.8 %convert_reduce_fusion.7 = (f32[768]{0:T(1024)}, bf16[1024,768]{1,0:T(8,128)(2,1)}, bf16[1024,768]{1,0:T(8,128)(2,1)S(1)}, bf16[1024,768]{1,0:T(8,128)(2,1)S(1)}, f32[768]{0:T(1024)}, /*index=5*/bf16[1024,768]{1,0:T(8,128)(2,1)}) fusion(f32[1024,768]{1,0:T(8,128)S(1)} %get-tuple-element.99, f32[1024,768]{1,0:T(8,128)S(1)} %fusion.233, ...), kind=kLoop, calls=%fused_computation.59 | loop fusion | flops 51902976 | bytes 25175040 | tf_op jit(solution)/shard_map/reduce_sum | solution.py:405
  296.1 18.9 %collective-permute-done.11 = bf16[1024,768]{1,0:T(8,128)(2,1)} collective-permute-done((bf16[1024,768]{1,0:T(8,128)(2,1)S(1)}, bf16[1024,768]{1,0:T(8,128)(2,1)}, u32[]{:S(2)}, u32[]{:S(2)}) %collective-permute-start.11) | collective-permute-done | bytes 1572896 | tf_op jit(solution)/shard_map/ppermute | solution.py:198
  317.8 29.0 %collective-permute-done.17 = bf16[1024,768]{1,0:T(8,128)(2,1)} collective-permute-done((bf16[1024,768]{1,0:T(8,128)(2,1)}, bf16[1024,768]{1,0:T(8,128)(2,1)}, u32[]{:S(2)}, u32[]{:S(2)}) %collective-permute-start.17) | collective-permute-done | bytes 1572896 | tf_op jit(solution)/shard_map/ppermute | solution.py:198
  349.7 4.6 fusion.117
  357.1 4.6 fusion.236
  365.2 5.4 fusion.94
  374.0 4.0 multiply_add_fusion.3
  378.0 5.6 fusion.31
  392.4 4.2 multiply_add_fusion.1
  399.1 4.1 convert_reduce_fusion.11
  406.2 9.8 %fusion.42.grad_ref = f32[1024,768]{1,0:T(8,128)} fusion(f32[1024,384]{0,1:T(8,128)S(1)} %copy-done.42, f32[1024,384]{0,1:T(8,128)} %get-tuple-element.115, f32[1024,384]{0,1:T(8,128)S(1)} %copy-done.41, f32[1024,384]{0,1:T(8,128)S(1)} %copy-done.40, f32[1024,384]{0,1:T(8,128)} %get-tuple-element.110, f32[1024,384]{0,1:T(8,128)} %get-tuple-element.111, ...), kind=kOutput, calls=%fused_computation.86 | convolution fusion | flops 3243769856 | bytes 19922944 | tf_op jit(solution)/shard_map/dot_general | solution.py:32
  416.0 34.6 %state_grad.1 = (f32[2,1,384]{2,1,0:T(1,128)}, f32[2,64,384]{2,1,0:T(8,128)}, f32[2,64,384]{2,1,0:T(8,128)}) custom-call(f32[2,1,384]{2,1,0:T(1,128)} %broadcast_in_dim.2.delta_ref, f32[2,64,384]{2,1,0:T(8,128)} %bitcast.279, f32[2,64,384]{2,1,0:T(8,128)} %bitcast.281, f32[1024,768]{1,0:T(8,128)} %fusion.42.grad_ref), custom_call_target="tpu_custom_call" | custom-call | tf_op jit(solution)/shard_map/state_grad/pallas_call | solution.py:146
  452.9 8.8 %convert_reduce_fusion.10 = (f32[384]{0:T(512)}, bf16[1024,384]{1,0:T(8,128)(2,1)S(1)}) fusion(f32[1024,768]{1,0:T(8,128)} %copy-done.21, f32[384]{0:T(512)S(1)} %get-tuple-element.89, f32[384]{0:T(512)S(1)} %get-tuple-element.88, f32[1024,384]{0,1:T(8,128)} %get-tuple-element.107, f32[1024,384]{0,1:T(8,128)} %get-tuple-element.106, ...), kind=kOutput, calls=%fused_computation.161 | convolution fusion | flops 1631190656 | bytes 12853760 | tf_op jit(solution)/shard_map/dot_general | solution.py:32
  525.6 62.5 %reduce-scatter.6.cloned.1.call-done = bf16[96,384]{1,0:T(8,128)(2,1)} async-done(((bf16[768,384]{1,0:T(8,128)(2,1)}), bf16[96,384]{1,0:T(8,128)(2,1)}) %reduce-scatter.6.cloned.1.call-update) | async-done | bytes 73744 | tf_op jit(solution)/shard_map/reduce_scatter | solution.py:419
  589.7 70.5 %reduce-scatter.10.cloned.1.call-done = bf16[96,1536]{1,0:T(8,128)(2,1)} async-done(((bf16[768,1536]{1,0:T(8,128)(2,1)}), bf16[96,1536]{1,0:T(8,128)(2,1)}) %reduce-scatter.10.cloned.1.call-update) | async-done | bytes 294928
  665.0 4.7 fusion.69
  683.1 37.1 %psum.14 = f32[5760]{0:T(1024)S(1)} all-reduce(f32[5760]{0:T(1024)} %constant_dynamic-update-slice_fusion.2), channel_id=1, replica_groups=mesh['dp'=8,'tensor'=4] {'dp'}, use_global_device_ids=true, to_apply=%region_26.27 | all-reduce | flops 5760 | bytes 46080 | tf_op jit(solution)/shard_map/psum | solution.py:427
  737.3 22.2 %reduce-scatter.8.cloned.1.call-done = bf16[384,768]{1,0:T(8,128)(2,1)} async-done(((bf16[3072,768]{1,0:T(8,128)(2,1)}), bf16[384,768]{1,0:T(8,128)(2,1)}) %reduce-scatter.8.cloned.1.call-update) | async-done | bytes 589840 | tf_op jit(solution)/shard_map/reduce_scatter | solution.py:418
  (413 shorter events, 227.8 us)
Async XLA Ops:
  7.2 84.8 %all-gather.4.cloned.1.call-start = ((), (), s32[]{:S(2)}) async-start(), calls=%async_computation.3 | async-start | bytes 1990656 | tf_op jit(solution)/shard_map/all_gather | solution.py:228
  9.0 132.8 %all-gather.6.cloned.1.call-start = ((), (), s32[]{:S(2)}) async-start(), calls=%async_computation.4 | async-start | bytes 5308416 | tf_op jit(solution)/shard_map/all_gather | solution.py:230
  11.0 177.9 %all-gather.8.cloned.1.call-start = ((), (), s32[]{:S(2)}) async-start(), calls=%async_computation.5 | async-start | bytes 1327104 | tf_op jit(solution)/shard_map/all_gather | solution.py:231
  11.7 512.1 %all-reduce.2.cloned.1.call-start = ((), (), s32[]{:S(2)}) async-start(), calls=%async_computation.8 | async-start | bytes 786432 | tf_op jit(solution)/shard_map/psum | solution.py:428
  168.4 25.2 %collective-permute-start = (bf16[1024,1536]{1,0:T(8,128)(2,1)}, bf16[1024,1536]{1,0:T(8,128)(2,1)}, u32[]{:S(2)}, u32[]{:S(2)}) collective-permute-start(bf16[1024,1536]{1,0:T(8,128)(2,1)} %convolution_convert_fusion.1), channel_id=1, source_target_pairs={{0,1},{1,0},{2,3},{3,2},{4,5},{5,4},{6,7},{7,6},{8,9},{9,8},{10,11... | collective-permute-start | bytes 9437192 | tf_op jit(solution)/shard_map/ppermute | solution.py:195
  173.3 25.1 %collective-permute-start.5 = (bf16[1024,1536]{1,0:T(8,128)(2,1)}, bf16[1024,1536]{1,0:T(8,128)(2,1)}, u32[]{:S(2)}, u32[]{:S(2)}) collective-permute-start(bf16[1024,1536]{1,0:T(8,128)(2,1)} %convolution_convert_fusion), channel_id=1, source_target_pairs={{0,1},{1,0},{2,3},{3,2},{4,5},{5,4},{6,7},{7,6},{8,9},{9,8},{10,11... | collective-permute-start | bytes 9437192 | tf_op jit(solution)/shard_map/ppermute | solution.py:195
  196.8 37.3 %collective-permute-start.1 = (bf16[1024,768]{1,0:T(8,128)(2,1)S(1)}, bf16[1024,768]{1,0:T(8,128)(2,1)S(1)}, u32[]{:S(2)}, u32[]{:S(2)}) collective-permute-start(bf16[1024,768]{1,0:T(8,128)(2,1)S(1)} %add_convert_fusion.1), channel_id=1, source_target_pairs={{0,2},{1,3},{2,0},{3,1},{4,6},{5,7},{6,4},{7,5},{8,10},{9,11},{10,... | collective-permute-start | bytes 4718600 | tf_op jit(solution)/shard_map/ppermute | solution.py:198
  201.3 65.8 %collective-permute-start.6 = (bf16[1024,768]{1,0:T(8,128)(2,1)S(1)}, bf16[1024,768]{1,0:T(8,128)(2,1)}, u32[]{:S(2)}, u32[]{:S(2)}) collective-permute-start(bf16[1024,768]{1,0:T(8,128)(2,1)S(1)} %add_convert_fusion), channel_id=1, source_target_pairs={{0,2},{1,3},{2,0},{3,1},{4,6},{5,7},{6,4},{7,5},{8,10},{9,11},{10,... | collective-permute-start | bytes 4718600 | tf_op jit(solution)/shard_map/ppermute | solution.py:198
  277.6 37.4 %collective-permute-start.11 = (bf16[1024,768]{1,0:T(8,128)(2,1)S(1)}, bf16[1024,768]{1,0:T(8,128)(2,1)}, u32[]{:S(2)}, u32[]{:S(2)}) collective-permute-start(bf16[1024,768]{1,0:T(8,128)(2,1)S(1)} %get-tuple-element.98), channel_id=1, source_target_pairs={{0,2},{1,3},{2,0},{3,1},{4,6},{5,7},{6,4},{7,5},{8,10},{9,11},{10,... | collective-permute-start | bytes 4718600 | tf_op jit(solution)/shard_map/ppermute | solution.py:198
  279.1 75.2 %collective-permute-start.10 = (bf16[1024,768]{1,0:T(8,128)(2,1)S(1)}, bf16[1024,768]{1,0:T(8,128)(2,1)}, u32[]{:S(2)}, u32[]{:S(2)}) collective-permute-start(bf16[1024,768]{1,0:T(8,128)(2,1)S(1)} %get-tuple-element.98), channel_id=1, source_target_pairs={{0,1},{1,0},{2,3},{3,2},{4,5},{5,4},{6,7},{7,6},{8,9},{9,8},{10,11... | collective-permute-start | bytes 4718600 | tf_op jit(solution)/shard_map/ppermute | solution.py:195
  279.1 67.8 %collective-permute-start.17 = (bf16[1024,768]{1,0:T(8,128)(2,1)}, bf16[1024,768]{1,0:T(8,128)(2,1)}, u32[]{:S(2)}, u32[]{:S(2)}) collective-permute-start(bf16[1024,768]{1,0:T(8,128)(2,1)} %get-tuple-element.192), channel_id=1, source_target_pairs={{0,2},{1,3},{2,0},{3,1},{4,6},{5,7},{6,4},{7,5},{8,10},{9,11},{10,... | collective-permute-start | bytes 4718600 | tf_op jit(solution)/shard_map/ppermute | solution.py:198
  279.6 77.5 %collective-permute-start.16 = (bf16[1024,768]{1,0:T(8,128)(2,1)}, bf16[1024,768]{1,0:T(8,128)(2,1)}, u32[]{:S(2)}, u32[]{:S(2)}) collective-permute-start(bf16[1024,768]{1,0:T(8,128)(2,1)} %get-tuple-element.192), channel_id=1, source_target_pairs={{0,1},{1,0},{2,3},{3,2},{4,5},{5,4},{6,7},{7,6},{8,9},{9,8},{10,11... | collective-permute-start | bytes 4718600 | tf_op jit(solution)/shard_map/ppermute | solution.py:195
  314.9 46.8 %collective-permute-start.12 = (bf16[1024,768]{1,0:T(8,128)(2,1)}, bf16[1024,768]{1,0:T(8,128)(2,1)S(1)}, u32[]{:S(2)}, u32[]{:S(2)}) collective-permute-start(bf16[1024,768]{1,0:T(8,128)(2,1)} %collective-permute-done.11), channel_id=1, source_target_pairs={{0,1},{1,0},{2,3},{3,2},{4,5},{5,4},{6,7},{7,6},{8,9},{9,8},{10,11... | collective-permute-start | bytes 4718600 | tf_op jit(solution)/shard_map/ppermute | solution.py:195
  317.3 196.1 %collective-permute-start.2 = (bf16[512,768]{1,0:T(8,128)(2,1)}, bf16[512,768]{1,0:T(8,128)(2,1)}, u32[]{:S(2)}, u32[]{:S(2)}) collective-permute-start(bf16[512,768]{1,0:T(8,128)(2,1)} %dynamic-slice_convert_fusion.3), channel_id=1, source_target_pairs={{0,1},{1,0},{2,3},{3,2},{4,5},{5,4},{6,7},{7,6},{8,9},{9,8},{10,11... | collective-permute-start | bytes 2359304 | tf_op jit(solution)/shard_map/ppermute | solution.py:195
  346.9 31.2 %collective-permute-start.18 = (bf16[1024,768]{1,0:T(8,128)(2,1)}, bf16[1024,768]{1,0:T(8,128)(2,1)}, u32[]{:S(2)}, u32[]{:S(2)}) collective-permute-start(bf16[1024,768]{1,0:T(8,128)(2,1)} %collective-permute-done.17), channel_id=1, source_target_pairs={{0,1},{1,0},{2,3},{3,2},{4,5},{5,4},{6,7},{7,6},{8,9},{9,8},{10,11... | collective-permute-start | bytes 4718600 | tf_op jit(solution)/shard_map/ppermute | solution.py:195
  452.4 135.7 %reduce-scatter.6.cloned.1.call-start = ((), (), s32[]{:S(2)}) async-start(), calls=%async_computation.6 | async-start | bytes 663552 | tf_op jit(solution)/shard_map/reduce_scatter | solution.py:419
  464.7 195.5 %reduce-scatter.10.cloned.1.call-start = ((), (), s32[]{:S(2)}) async-start(), calls=%async_computation.9 | async-start | bytes 2654208
  472.6 286.9 %reduce-scatter.8.cloned.1.call-start = ((), (), s32[]{:S(2)}) async-start(), calls=%async_computation.7 | async-start | bytes 5308416 | tf_op jit(solution)/shard_map/reduce_scatter | solution.py:418
  477.3 39.4 %collective-permute-start.7 = (bf16[512,768]{1,0:T(8,128)(2,1)}, bf16[512,768]{1,0:T(8,128)(2,1)}, u32[]{:S(2)}, u32[]{:S(2)}) collective-permute-start(bf16[512,768]{1,0:T(8,128)(2,1)} %dynamic-slice_convert_fusion.2), channel_id=1, source_target_pairs={{0,1},{1,0},{2,3},{3,2},{4,5},{5,4},{6,7},{7,6},{8,9},{9,8},{10,11... | collective-permute-start | bytes 2359304 | tf_op jit(solution)/shard_map/ppermute | solution.py:195
  505.7 5.0 collective-permute-start.13
  510.3 10.4 %collective-permute-start.19 = (bf16[512,768]{1,0:T(8,128)(2,1)}, bf16[512,768]{1,0:T(8,128)(2,1)}, u32[]{:S(2)}, u32[]{:S(2)}) collective-permute-start(bf16[512,768]{1,0:T(8,128)(2,1)} %dynamic-slice_convert_fusion), channel_id=1, source_target_pairs={{0,1},{1,0},{2,3},{3,2},{4,5},{5,4},{6,7},{7,6},{8,9},{9,8},{10,11... | collective-permute-start | bytes 2359304 | tf_op jit(solution)/shard_map/ppermute | solution.py:195
  511.9 150.5 %collective-permute-start.14 = (bf16[512,768]{1,0:T(8,128)(2,1)}, bf16[512,768]{1,0:T(8,128)(2,1)}, u32[]{:S(2)}, u32[]{:S(2)}) collective-permute-start(bf16[512,768]{1,0:T(8,128)(2,1)} %add_convert_fusion.9), channel_id=1, source_target_pairs={{0,2},{1,3},{2,0},{3,1},{4,6},{5,7},{6,4},{7,5},{8,10},{9,11},{10,... | collective-permute-start | bytes 2359304 | tf_op jit(solution)/shard_map/ppermute | solution.py:198
  515.7 149.3 %collective-permute-start.3 = (bf16[512,768]{1,0:T(8,128)(2,1)}, bf16[512,768]{1,0:T(8,128)(2,1)}, u32[]{:S(2)}, u32[]{:S(2)}) collective-permute-start(bf16[512,768]{1,0:T(8,128)(2,1)} %add_convert_fusion.11), channel_id=1, source_target_pairs={{0,2},{1,3},{2,0},{3,1},{4,6},{5,7},{6,4},{7,5},{8,10},{9,11},{10,... | collective-permute-start | bytes 2359304 | tf_op jit(solution)/shard_map/ppermute | solution.py:198
  519.0 150.8 %collective-permute-start.8 = (bf16[512,768]{1,0:T(8,128)(2,1)}, bf16[512,768]{1,0:T(8,128)(2,1)}, u32[]{:S(2)}, u32[]{:S(2)}) collective-permute-start(bf16[512,768]{1,0:T(8,128)(2,1)} %add_convert_fusion.10), channel_id=1, source_target_pairs={{0,2},{1,3},{2,0},{3,1},{4,6},{5,7},{6,4},{7,5},{8,10},{9,11},{10,... | collective-permute-start | bytes 2359304 | tf_op jit(solution)/shard_map/ppermute | solution.py:198
  522.9 139.6 %copy-start.66 = (f32[512]{0:T(512)S(1)}, f32[512]{0:T(512)}, u32[]{:S(2)}) copy-start(f32[512]{0:T(512)} %copy-done.65) | copy-start | bytes 6148
  522.9 139.6 %copy-start.68 = (f32[512]{0:T(512)S(1)}, f32[512]{0:T(512)}, u32[]{:S(2)}) copy-start(f32[512]{0:T(512)} %add_rsqrt_fusion.3) | copy-start | bytes 6148
  522.9 142.1 %collective-permute-start.20 = (bf16[512,768]{1,0:T(8,128)(2,1)}, bf16[512,768]{1,0:T(8,128)(2,1)}, u32[]{:S(2)}, u32[]{:S(2)}) collective-permute-start(bf16[512,768]{1,0:T(8,128)(2,1)} %add_convert_fusion.8), channel_id=1, source_target_pairs={{0,2},{1,3},{2,0},{3,1},{4,6},{5,7},{6,4},{7,5},{8,10},{9,11},{10,... | collective-permute-start | bytes 2359304 | tf_op jit(solution)/shard_map/ppermute | solution.py:198
  672.6 56.5 %collective-permute-start.21 = (bf16[512,768]{1,0:T(8,128)(2,1)S(1)}, bf16[512,768]{1,0:T(8,128)(2,1)S(1)}, u32[]{:S(2)}, u32[]{:S(2)}) collective-permute-start(bf16[512,768]{1,0:T(8,128)(2,1)S(1)} %get-tuple-element.142), channel_id=1, source_target_pairs={{0,1},{1,0},{2,3},{3,2},{4,5},{5,4},{6,7},{7,6},{8,9},{9,8},{10,11... | collective-permute-start | bytes 2359304 | tf_op jit(solution)/shard_map/ppermute | solution.py:195
  721.5 6.3 collective-permute-start.22
  721.5 7.7 %collective-permute-start.9 = (bf16[512,768]{1,0:T(8,128)(2,1)S(1)}, bf16[512,768]{1,0:T(8,128)(2,1)}, u32[]{:S(2)}, u32[]{:S(2)}) collective-permute-start(bf16[512,768]{1,0:T(8,128)(2,1)S(1)} %get-tuple-element.143), channel_id=1, source_target_pairs={{0,1},{1,0},{2,3},{3,2},{4,5},{5,4},{6,7},{7,6},{8,9},{9,8},{10,11... | collective-permute-start | bytes 2359304 | tf_op jit(solution)/shard_map/ppermute | solution.py:195
  727.2 3.4 collective-permute-start.15
  727.2 4.8 collective-permute-start.4
  (104 other events, 799.1 us)
Sparse Core Ops, SparseCore 0:
  10.8 48.9 all-gather.3
  62.4 79.3 all-gather.5
  143.9 39.2 all-gather.7
  452.5 70.0 all-reduce.1
  526.3 61.7 reduce-scatter.5
  591.5 68.6 reduce-scatter.9
  663.8 95.5 reduce-scatter.7

commit v2 on v1

v2 whole, which is shorter than its diff:
```python
import functools
import math

import jax
import jax.numpy as jnp
import numpy as np
from jax import lax
from jax.experimental import pallas as pl
from jax.experimental.pallas import tpu as pltpu
from jax.sharding import PartitionSpec as P

EPSILON = 1e-05
LANES = 128
INNER = 32
BAND = 256
ROWS = 256
BF = jnp.bfloat16
F32 = jnp.float32
GELU_C = math.sqrt(2.0 / math.pi)
GELU_A = 0.044715


def gelu_pair(x):
    square = x * x
    bend = jnp.tanh(GELU_C * x * (1.0 + GELU_A * square))
    half = 0.5 * (1.0 + bend)
    slope = half + 0.5 * x * (1.0 - bend * bend) * (GELU_C * (1.0 + 3.0 * GELU_A * square))
    return x * half, slope


def after(value, *others):
    return lax.optimization_barrier((value,) + others)[0]


def dot_nt(a, b):
    return lax.dot_general(a, b, (((1,), (1,)), ((), ())), preferred_element_type=F32)


def dot_tn(a, b):
    return lax.dot_general(a, b, (((0,), (0,)), ((), ())), preferred_element_type=F32)


def dot_nn(a, b):
    return jnp.dot(a, b, preferred_element_type=F32)


def fill_powers(rate_ref, one_ref, many_ref, scale):
    states = rate_ref.shape[0]
    offset = lax.broadcasted_iota(jnp.int32, (INNER, LANES), 0).astype(F32)

    def body(n, _):
        row = rate_ref[pl.ds(n, 1), :]
        one_ref[n] = jnp.exp(-(row * offset))
        wide = jnp.exp(-(row * (offset * float(INNER))))
        if scale is not None:
            wide = wide * scale[pl.ds(n, 1), :]
        many_ref[n] = wide
        return 0

    lax.fori_loop(0, states, body, 0)


def impulse_kernel(delta_ref, rate_ref, readout_ref, out_ref, a_ref, w_ref, one_ref, many_ref):
    states = rate_ref.shape[1]
    length = out_ref.shape[0]
    step = jnp.exp(delta_ref[0])
    a_ref[...] = step * rate_ref[0]
    w_ref[...] = step * readout_ref[0]
    fill_powers(a_ref, one_ref, many_ref, w_ref)
    group = 8
    for start in range(0, length // INNER, group):

        def body(n, sums):
            base = one_ref[n]
            return tuple(
                total + many_ref[n, start + j : start + j + 1, :] * base
                for j, total in enumerate(sums)
            )

        sums = lax.fori_loop(
            0, states, body, tuple(jnp.zeros((INNER, LANES), F32) for _ in range(group))
        )
        for j, total in enumerate(sums):
            at = (start + j) * INNER
            out_ref[at : at + INNER, :] = total.astype(out_ref.dtype)


def impulse(delta, rate, readout, length, c):
    dirs, states, channels = rate.shape
    lanes = channels // LANES
    spec = pl.BlockSpec((1, states, LANES), lambda j: (c, 0, j))
    return pl.pallas_call(
        impulse_kernel,
        name="impulse",
        grid=(lanes,),
        in_specs=[pl.BlockSpec((1, 1, LANES), lambda j: (c, 0, j)), spec, spec],
        out_specs=pl.BlockSpec((length, LANES), lambda j: (0, j)),
        out_shape=jax.ShapeDtypeStruct((length, channels), BF),
        scratch_shapes=[
            pltpu.VMEM((states, LANES), F32),
            pltpu.VMEM((states, LANES), F32),
            pltpu.VMEM((states, INNER, LANES), F32),
            pltpu.VMEM((states, length // INNER, LANES), F32),
        ],
    )(delta, rate, readout)


def state_grad_kernel(
    delta_ref, rate_ref, readout_ref, grad_ref, gdelta_ref, grate_ref, greadout_ref, a_ref, one_ref, many_ref, g_ref, m_ref
):
    states = rate_ref.shape[1]
    length = grad_ref.shape[0]
    step = jnp.exp(delta_ref[0])
    a_ref[...] = step * rate_ref[0]
    fill_powers(a_ref, one_ref, many_ref, None)
    offset = lax.broadcasted_iota(jnp.int32, (INNER, LANES), 0).astype(F32)
    group = 4
    zero = jnp.zeros((INNER, LANES), F32)

    def body(i, _):
        sums = [zero] * group
        moments = [zero] * group
        for k in range(length // INNER - 1, -1, -1):
            block = grad_ref[k * INNER : (k + 1) * INNER, :]
            for j in range(group):
                sums[j] = sums[j] + many_ref[i * group + j, k : k + 1, :] * block
                if k > 0:
                    moments[j] = moments[j] + sums[j]
        for j in range(group):
            n = i * group + j
            base = one_ref[n]
            g_ref[pl.ds(n, 1), :] = jnp.sum(base * sums[j], axis=0, keepdims=True)
            m_ref[pl.ds(n, 1), :] = jnp.sum(
                base * (offset * sums[j] + float(INNER) * moments[j]), axis=0, keepdims=True
            )
        return 0

    lax.fori_loop(0, states // group, body, 0)
    rate = rate_ref[0]
    readout = readout_ref[0]
    grad_w = g_ref[...]
    grad_a = -(step * readout) * m_ref[...]
    greadout_ref[0] = step * grad_w
    grate_ref[0] = step * grad_a
    gdelta_ref[0] = step * jnp.sum(readout * grad_w + rate * grad_a, axis=0, keepdims=True)


def state_grad(delta, rate, readout, grad, c):
    dirs, states, channels = rate.shape
    length = grad.shape[0]
    lanes = channels // LANES
    spec = pl.BlockSpec((1, states, LANES), lambda j: (c, 0, j))
    row = pl.BlockSpec((1, 1, LANES), lambda j: (c, 0, j))
    out_spec = pl.BlockSpec((1, states, LANES), lambda j: (0, 0, j))
    out_row = pl.BlockSpec((1, 1, LANES), lambda j: (0, 0, j))
    return pl.pallas_call(
        state_grad_kernel,
        name="state_grad",
        grid=(lanes,),
        in_specs=[row, spec, spec, pl.BlockSpec((length, LANES), lambda j: (0, c * lanes + j))],
        out_specs=[out_row, out_spec, out_spec],
        out_shape=[
            jax.ShapeDtypeStruct((1, 1, channels), F32),
            jax.ShapeDtypeStruct((1, states, channels), F32),
            jax.ShapeDtypeStruct((1, states, channels), F32),
        ],
        scratch_shapes=[
            pltpu.VMEM((states, LANES), F32),
            pltpu.VMEM((states, INNER, LANES), F32),
            pltpu.VMEM((states, length // INNER, LANES), F32),
            pltpu.VMEM((states, LANES), F32),
            pltpu.VMEM((states, LANES), F32),
        ],
    )(delta, rate, readout, grad)


def whole(shape):
    return pl.BlockSpec(shape, lambda *at: (0,) * len(shape), pipeline_mode=pl.Buffered(1))


def out(shape):
    return pl.BlockSpec(shape, lambda *at: (0,) * len(shape))


def by_rows(width):
    return pl.BlockSpec((ROWS, width), lambda i, *at: (i, 0))


def response_kernel(first_ref, second_ref, rows_ref, turn_ref, k_ref):
    channels = first_ref.shape[1]
    length = first_ref.shape[0]
    tile = lambda v: jnp.concatenate([v] * (channels // LANES), axis=1)
    c, s = tile(turn_ref[0]), tile(turn_ref[1])
    for i, ref in enumerate((first_ref, second_ref)):
        f = dot_nn(rows_ref[...], ref[...]) * (1.0 / length)
        p, q = f[:BAND], f[BAND:]
        at = slice(i * channels, (i + 1) * channels)
        k_ref[0, 0, :, at] = c * p + s * q
        k_ref[0, 1, :, at] = c * q - s * p


def response(first, second, rows, turn):
    length, channels = first.shape
    bands = length // BAND
    return pl.pallas_call(
        response_kernel,
        name="response",
        grid=(bands,),
        in_specs=[
            whole((length, channels)),
            whole((length, channels)),
            pl.BlockSpec((2 * BAND, length), lambda b: (b, 0)),
            pl.BlockSpec((2, BAND, LANES), lambda b: (0, b, 0)),
        ],
        out_specs=pl.BlockSpec((1, 2, BAND, 2 * channels), lambda b: (b, 0, 0, 0)),
        out_shape=jax.ShapeDtypeStruct((bands, 2, BAND, 2 * channels), F32),
        compiler_params=pltpu.CompilerParams(vmem_limit_bytes=56 << 20),
    )(first, second, rows, turn)


def response_grad_kernel(lag_ref, cols_ref, turn_ref, out_ref):
    length, channels = out_ref.shape
    tile = lambda v: jnp.concatenate([v] * (channels // LANES), axis=1)
    c, s = tile(turn_ref[0]) * (1.0 / length), tile(turn_ref[1]) * (1.0 / length)
    p, q = lag_ref[:BAND], lag_ref[BAND:]
    turned = jnp.concatenate([(c * p - s * q).astype(BF), (s * p + c * q).astype(BF)], axis=0)
    step = dot_nn(cols_ref[...], turned)

    @pl.when(pl.program_id(0) == 0)
    def _():
        out_ref[...] = step

    @pl.when(pl.program_id(0) > 0)
    def _():
        out_ref[...] += step


def response_grad(lag, cols, turn):
    length = cols.shape[0]
    channels = lag.shape[1]
    return pl.pallas_call(
        response_grad_kernel,
        name="response_grad",
        grid=(length // BAND,),
        in_specs=[
            pl.BlockSpec((2 * BAND, channels), lambda b: (b, 0)),
            pl.BlockSpec((length, 2 * BAND), lambda b: (0, b)),
            pl.BlockSpec((2, BAND, LANES), lambda b: (0, b, 0)),
        ],
        out_specs=out((length, channels)),
        out_shape=jax.ShapeDtypeStruct((length, channels), F32),
        compiler_params=pltpu.CompilerParams(vmem_limit_bytes=56 << 20),
    )(lag, cols, turn)


def send_kernel(a_ref, first_ref, second_ref, first_out, second_out):
    first_out[...] = dot_nn(a_ref[...], first_ref[...]).astype(BF)
    second_out[...] = dot_nn(a_ref[...], second_ref[...]).astype(BF)


def send(a, first, second):
    length, width = a.shape
    n = first.shape[1]
    return pl.pallas_call(
        send_kernel,
        name="send",
        grid=(length // ROWS,),
        in_specs=[by_rows(width), whole((width, n)), whole((width, n))],
        out_specs=[by_rows(n), by_rows(n)],
        out_shape=[jax.ShapeDtypeStruct((length, n), BF)] * 2,
    )(a, first, second)


def join_kernel(a_ref, b_ref, add_ref, out_ref):
    out_ref[...] = (dot_nn(a_ref[...], b_ref[...]) + add_ref[...].astype(F32)).astype(BF)


def join(a, b, add):
    length, width = a.shape
    n = b.shape[1]
    return pl.pallas_call(
        join_kernel,
        name="join",
        grid=(length // ROWS,),
        in_specs=[by_rows(width), whole((width, n)), by_rows(n)],
        out_specs=by_rows(n),
        out_shape=jax.ShapeDtypeStruct((length, n), BF),
    )(a, b, add)


def before_gate_kernel(
    slot, length_ref, both_ref, mix_ref, near_ref, mix_bias_ref, normed_ref, value_ref, value_bias_ref,
    cot_ref, out_ref, part_ref, act_ref, first_ref, second_ref, up_ref, sum_ref,
):
    i = pl.program_id(0)
    part_ref[...] = dot_nn(both_ref[...], mix_ref[...]) + near_ref[...].astype(F32) + mix_bias_ref[...]
    act, slope = gelu_pair(dot_nn(normed_ref[...], value_ref[...]) + value_bias_ref[...])
    cot = cot_ref[0].astype(F32)
    time_at = lax.broadcasted_iota(jnp.int32, cot.shape, 0) + i * ROWS
    upstream = jnp.where(time_at < length_ref[slot], cot, 0.0)
    low = upstream.astype(BF)
    grad_hidden = dot_nn(low, out_ref[...])
    act_ref[...] = act
    first_ref[...] = grad_hidden * act
    second_ref[...] = grad_hidden * slope
    up_ref[...] = low

    @pl.when(i == 0)
    def _():
        sum_ref[...] = jnp.zeros_like(sum_ref)

    sum_ref[...] += jnp.sum(upstream, axis=0, keepdims=True)


def before_gate(both, mix, near, mix_bias, normed, last_all, value_bias, cotangent, lengths, slot):
    length, width = normed.shape
    n = mix.shape[1]
    return pl.pallas_call(
        functools.partial(before_gate_kernel, slot),
        name="before_gate",
        grid_spec=pltpu.PrefetchScalarGridSpec(
            num_scalar_prefetch=1,
            grid=(length // ROWS,),
            in_specs=[
                by_rows(both.shape[1]),
                whole(mix.shape),
                by_rows(n),
                whole((1, n)),
                by_rows(width),
                whole((width, n)),
                whole((1, n)),
                pl.BlockSpec((1, ROWS, width), lambda i, *at: (slot, i, 0)),
                pl.BlockSpec((width, n), lambda *at: (0, 1), pipeline_mode=pl.Buffered(1)),
            ],
            out_specs=[by_rows(n)] * 4 + [by_rows(width), out((1, width))],
        ),
        out_shape=[jax.ShapeDtypeStruct((length, n), F32)] * 4
        + [jax.ShapeDtypeStruct((length, width), BF), jax.ShapeDtypeStruct((1, width), F32)],
        compiler_params=pltpu.CompilerParams(vmem_limit_bytes=56 << 20),
    )(lengths, both, mix, near, mix_bias, normed, last_all, value_bias, cotangent, last_all)


def gate_kernel(part_ref, far_ref, act_ref, first_ref, second_ref, hidden_ref, gate_ref, value_ref, sum_ref):
    gate_act, gate_slope = gelu_pair(part_ref[...] + far_ref[...].astype(F32))
    hidden_ref[...] = (gate_act * act_ref[...]).astype(BF)
    gate = (gate_slope * first_ref[...]).astype(BF)
    value = (gate_act * second_ref[...]).astype(BF)
    gate_ref[...] = gate
    value_ref[...] = value

    @pl.when(pl.program_id(0) == 0)
    def _():
        sum_ref[...] = jnp.zeros_like(sum_ref)

    sum_ref[0:1, :] += jnp.sum(gate.astype(F32), axis=0, keepdims=True)
    sum_ref[1:2, :] += jnp.sum(value.astype(F32), axis=0, keepdims=True)


def gate(part, far, act, first, second):
    length, n = part.shape
    return pl.pallas_call(
        gate_kernel,
        name="gate",
        grid=(length // ROWS,),
        in_specs=[by_rows(n)] * 5,
        out_specs=[by_rows(n)] * 3 + [out((2, n))],
        out_shape=[jax.ShapeDtypeStruct((length, n), BF)] * 3 + [jax.ShapeDtypeStruct((2, n), F32)],
        compiler_params=pltpu.CompilerParams(vmem_limit_bytes=56 << 20),
    )(part, far, act, first, second)


def tables(length):
    odd = 2 * np.arange(length, dtype=np.int64) + 1
    angle = (odd[:, None] * odd[None, :]) % (8 * length) * (math.pi / (4 * length))
    bands = length // BAND
    both = np.stack([np.cos(angle).reshape(bands, BAND, length), np.sin(angle).reshape(bands, BAND, length)], axis=1)
    rows = both.reshape(2 * length, length)
    turn = odd * (math.pi / (4 * length))
    return rows.astype(BF), np.ascontiguousarray(rows.T).astype(BF), np.repeat(
        np.stack([np.cos(turn), np.sin(turn)])[:, :, None], LANES, axis=2
    ).astype(np.float32)

def conv_forward_kernel(slot, length_ref, normed_ref, weight_ref, bias_ref, rows_ref, cols_ref, k_ref, skip_ref, slope_ref, low_ref, u_ref, both_ref, total_ref):
    band = pl.program_id(0)
    length, channels = slope_ref.shape

    @pl.when(band == 0)
    def _():
        def body(i, _):
            at = pl.ds(pl.multiple_of(i * 256, 256), 256)
            pre = dot_nn(normed_ref[at, :], weight_ref[...]) + bias_ref[...]
            value, slope = gelu_pair(pre)
            time_at = lax.broadcasted_iota(jnp.int32, pre.shape, 0) + i * 256
            live = jnp.where(time_at < length_ref[slot], 1.0, 0.0)
            signal = value * live
            slope_ref[at, :] = slope * live
            low_ref[at, :] = signal.astype(BF)
            total_ref[at, :channels] = skip_ref[0:1, :] * signal
            total_ref[at, channels:] = skip_ref[1:2, :] * signal
            return 0
        lax.fori_loop(0, length // 256, body, 0)

    u = dot_nn(rows_ref[...], low_ref[...])
    u_ref[...] = u
    uc, us = u[:BAND], u[BAND:]
    k0c, k1c = k_ref[0, 0, :, :channels], k_ref[0, 0, :, channels:]
    k0s, k1s = k_ref[0, 1, :, :channels], k_ref[0, 1, :, channels:]
    product = jnp.concatenate(
        [
            jnp.concatenate([uc * k0c - us * k0s, uc * k1c + us * k1s], axis=1).astype(BF),
            jnp.concatenate([uc * k0s + us * k0c, us * k1c - uc * k1s], axis=1).astype(BF),
        ],
        axis=0,
    )
    total_ref[...] += dot_nn(cols_ref[...], product)

    @pl.when(band == pl.num_programs(0) - 1)
    def _():
        both_ref[...] = total_ref[...].astype(BF)

def conv_forward(normed, weight, bias, k, skip, lengths, rows, cols, slot):
    length, width = normed.shape
    channels = weight.shape[1]
    bands = length // BAND
    return pl.pallas_call(
        functools.partial(conv_forward_kernel, slot),
        name="conv_forward",
        grid_spec=pltpu.PrefetchScalarGridSpec(
            num_scalar_prefetch=1,
            grid=(bands,),
            in_specs=[
                whole((length, width)), whole((width, channels)), whole((1, channels)),
                pl.BlockSpec((2 * BAND, length), lambda b, n: (b, 0)),
                pl.BlockSpec((length, 2 * BAND), lambda b, n: (0, b)),
                pl.BlockSpec((1, 2, BAND, 2 * channels), lambda b, n: (b, 0, 0, 0)),
                whole((2, channels)),
            ],
            out_specs=[
                out((length, channels)), out((length, channels)),
                pl.BlockSpec((2 * BAND, channels), lambda b, n: (b, 0)),
                out((length, 2 * channels)),
            ],
            scratch_shapes=[pltpu.VMEM((length, 2 * channels), F32)],
        ),
        out_shape=[
            jax.ShapeDtypeStruct((length, channels), F32),
            jax.ShapeDtypeStruct((length, channels), BF),
            jax.ShapeDtypeStruct((2 * length, channels), F32),
            jax.ShapeDtypeStruct((length, 2 * channels), BF),
        ],
        compiler_params=pltpu.CompilerParams(vmem_limit_bytes=56 << 20),
    )(lengths, normed, weight, bias, rows, cols, k, skip)

def conv_backward_kernel(count, *refs):
    pieces, mixes = refs[:count], refs[count:2 * count]
    rows_ref, cols_ref, k_ref, u_ref, slope_ref, low_ref, skip_ref, before_ref, feed_ref, lag_ref, skips_ref, both_ref, total_ref = refs[2 * count:]
    band = pl.program_id(0)
    length, channels = slope_ref.shape

    @pl.when(band == 0)
    def _():
        def body(i, sums):
            at = pl.ds(pl.multiple_of(i * 256, 256), 256)
            both = dot_nt(pieces[0][at, :], mixes[0][...])
            for piece, mix in zip(pieces[1:], mixes[1:]):
                both = both + dot_nt(piece[at, :], mix[...])
            both_ref[at, :] = both.astype(BF)
            total_ref[at, :] = skip_ref[0:1, :] * both[:, :channels] + skip_ref[1:2, :] * both[:, channels:]
            signal = low_ref[at, :].astype(F32)
            return sums + jnp.sum(both * jnp.concatenate([signal, signal], axis=1), axis=0, keepdims=True)
        skips_ref[...] = lax.fori_loop(0, length // 256, body, jnp.zeros((1, 2 * channels), F32))

    g = dot_nn(rows_ref[...], both_ref[...])
    ac, bc = g[:BAND, :channels], g[:BAND, channels:]
    as_, bs = g[BAND:, :channels], g[BAND:, channels:]
    uc, us = u_ref[:BAND], u_ref[BAND:]
    k0c, k1c = k_ref[0, 0, :, :channels], k_ref[0, 0, :, channels:]
    k0s, k1s = k_ref[0, 1, :, :channels], k_ref[0, 1, :, channels:]
    back = jnp.concatenate(
        [
            (ac * k0c + as_ * k0s + bc * k1c - bs * k1s).astype(BF),
            (as_ * k0c - ac * k0s + bc * k1s + bs * k1c).astype(BF),
        ],
        axis=0,
    )
    if before_ref is None:
        lag_ref[:BAND, :channels] = ac * uc + as_ * us
        lag_ref[:BAND, channels:] = uc * bc + us * bs
        lag_ref[BAND:, :channels] = as_ * uc - ac * us
        lag_ref[BAND:, channels:] = us * bc - uc * bs
    else:
        lag_ref[:BAND, :channels] = before_ref[:BAND, :channels] + ac * uc + as_ * us
        lag_ref[:BAND, channels:] = before_ref[:BAND, channels:] + uc * bc + us * bs
        lag_ref[BAND:, :channels] = before_ref[BAND:, :channels] + as_ * uc - ac * us
        lag_ref[BAND:, channels:] = before_ref[BAND:, channels:] + us * bc - uc * bs
    total_ref[...] += dot_nn(cols_ref[...], back)

    @pl.when(band == pl.num_programs(0) - 1)
    def _():
        feed_ref[...] = (slope_ref[...] * total_ref[...]).astype(BF)

def conv_backward(pieces, mixes, k, u, slope, low, skip, rows, cols, before):
    length, channels = slope.shape
    width = pieces[0].shape[1]
    bands = length // BAND
    band_spec = pl.BlockSpec((2 * BAND, 2 * channels), lambda b: (b, 0))
    count = len(pieces)
    def kernel(*refs):
        at = 2 * count + 7
        if before is None: refs = refs[:at] + (None,) + refs[at:]
        conv_backward_kernel(count, *refs)
    return pl.pallas_call(
        kernel,
        name="conv_backward",
        grid=(bands,),
        in_specs=[whole((length, width))] * count + [whole((2 * channels, width))] * count + [
            pl.BlockSpec((2 * BAND, length), lambda b: (b, 0)),
            pl.BlockSpec((length, 2 * BAND), lambda b: (0, b)),
            pl.BlockSpec((1, 2, BAND, 2 * channels), lambda b: (b, 0, 0, 0)),
            pl.BlockSpec((2 * BAND, channels), lambda b: (b, 0)),
            whole((length, channels)), whole((length, channels)), whole((2, channels)),
        ] + ([] if before is None else [band_spec]),
        out_specs=[out((length, channels)), band_spec, out((1, 2 * channels))],
        out_shape=[
            jax.ShapeDtypeStruct((length, channels), BF),
            jax.ShapeDtypeStruct((2 * length, 2 * channels), F32),
            jax.ShapeDtypeStruct((1, 2 * channels), F32),
        ],
        scratch_shapes=[pltpu.VMEM((length, 2 * channels), BF), pltpu.VMEM((length, channels), F32)],
        compiler_params=pltpu.CompilerParams(vmem_limit_bytes=60 << 20),
    )(*pieces, *mixes, rows, cols, k, u, slope, low, skip, *(() if before is None else (before,)))


def make_shards(dp_size, tensor_size):
    core_swap = [(i, i ^ 1) for i in range(tensor_size)]
    far_swap = [(i, i ^ 2) for i in range(tensor_size)]
    parts_of = dp_size // tensor_size

    def near(v):
        return lax.ppermute(v, "tensor", core_swap)

    def far(v):
        return lax.ppermute(v, "tensor", far_swap)

    def across(v, mask):
        return lax.ppermute(v, "dp", [(i, i ^ mask) for i in range(dp_size)])

    def shards(
        inputs,
        cotangent,
        lengths,
        norm_gain,
        norm_bias,
        value_weight,
        value_bias,
        feed_weight,
        feed_bias,
        mix_forward,
        mix_backward,
        mix_bias,
        out_weight,
        out_bias,
        state_delta,
        state_rate,
        state_readout,
        state_skip,
    ):
        slots, length, width = inputs.shape
        channels = feed_weight.shape[1]
        hidden_width = value_weight.shape[1]
        states = state_rate.shape[2]
        me = lax.axis_index("tensor")
        rank = lax.axis_index("dp")
        core = me % 2
        half = length // 2

        def collect(v):
            whole_v = v[None]
            mask = dp_size // 2
            stages = []
            while mask:
                stages.append(whole_v)
                other = across(whole_v, mask)
                upper = (rank & mask) != 0
                whole_v = jnp.stack(
                    [jnp.where(upper, other, whole_v), jnp.where(upper, whole_v, other)], axis=1
                )
                whole_v = whole_v.reshape((-1,) + v.shape)
                mask //= 2
            return whole_v.reshape((-1,) + v.shape[1:]), stages

        class Halving:
            def __init__(self, blocks):
                self.blocks = blocks
                self.give = None

            def launch(self, mask, flip=False):
                upper = ((rank & mask) != 0) ^ flip
                pairs = list(zip(self.blocks[::2], self.blocks[1::2]))
                self.give = jnp.concatenate(
                    [jnp.where(upper, a, b).astype(BF) for a, b in pairs], axis=0
                )
                self.blocks = [jnp.where(upper, b, a) for a, b in pairs]
                self.got = across(self.give, mask)
                return self

            def land(self, *anchors):
                got = after(self.got, *anchors)
                size = self.blocks[0].shape[0]
                self.blocks = [
                    b + got[i * size : (i + 1) * size].astype(F32) for i, b in enumerate(self.blocks)
                ]
                return self

        def row_blocks(v):
            size = v.shape[0] // dp_size
            return [v[i * size : (i + 1) * size] for i in range(dp_size)]

        def total_over_dp(v):
            mask = 1
            while mask < dp_size:
                v = v + across(v, mask)
                mask *= 2
            return v

        feed_full, feed_stages = collect(feed_weight)
        mix_own = jnp.concatenate([mix_forward, mix_backward], axis=0)
        mix_all = lax.all_gather(mix_own, "dp", axis=0, tiled=False)
        last_own = jnp.concatenate([value_weight, out_weight.T], axis=1)
        last_all = lax.all_gather(last_own, "dp", axis=0, tiled=True)
        mix_groups = mix_all.reshape((tensor_size, parts_of) + mix_own.shape)
        mix_of = []
        for j in range(tensor_size):
            quarter = lax.dynamic_index_in_dim(mix_groups, me ^ j, axis=0, keepdims=False)
            mix_of.append(jnp.concatenate([quarter[i] for i in range(parts_of)], axis=1))

        delta = state_delta[:, None, :]
        rate = jnp.swapaxes(state_rate, 1, 2)
        readout = jnp.swapaxes(state_readout, 1, 2)
        fourier_rows, fourier_cols, turn = (jnp.asarray(v) for v in tables(length))
        pulses = [
            impulse(after(delta, feed_stages[c - 2]), rate, readout, length, c) for c in range(2)
        ]
        spectra = response(pulses[0], pulses[1], fourier_rows, turn)

        time_at = jnp.arange(length)[:, None]
        normed, slope, low, u, both = [], [], [], [], []
        for slot in range(slots):
            rows = inputs[slot].astype(F32)
            center = rows - jnp.mean(rows, axis=-1, keepdims=True)
            spread = jnp.mean(center * center, axis=-1, keepdims=True)
            normed.append((center * lax.rsqrt(spread + EPSILON) * norm_gain + norm_bias).astype(BF))
        for slot in range(slots):
            parts = conv_forward(
                normed[slot],
                feed_full,
                feed_bias[None, :],
                spectra,
                state_skip,
                lengths,
                fourier_rows,
                fourier_cols,
                slot,
            )
            for whole_list, part in zip((slope, low, u, both), parts):
                whole_list.append(part)

        passed = None
        near_own, passes = [], []
        for slot in range(slots):
            left = both[slot] if passed is None else after(both[slot], passed)
            to_own, to_pass = send(left, mix_of[1], mix_of[3])
            passed = join(left, mix_of[2], near(to_pass))
            near_own.append(near(to_own))
            passes.append(passed)
        last_all = after(last_all, passed)
        pre = []
        for slot in range(slots):
            pre.append(
                before_gate(
                    both[slot],
                    mix_of[0],
                    near_own[slot],
                    mix_bias[None, :],
                    normed[slot],
                    last_all,
                    value_bias[None, :],
                    cotangent,
                    lengths,
                    slot,
                )
            )
        upstream_low = [p[4] for p in pre]
        value_full = last_all[:, :hidden_width]
        out_all = last_all[:, hidden_width:]

        hidden, grad_gate, grad_value, gate_sums = [], [], [], []
        for slot in range(slots):
            arrived = far(passes[slot])
            if slot == 0:
                arrived = after(arrived, pre[-1][0])
            else:
                arrived = after(arrived, grad_gate[-1])
            parts = gate(pre[slot][0], arrived, *pre[slot][1:4])
            for whole_list, part in zip((hidden, grad_gate, grad_value, gate_sums), parts):
                whole_list.append(part)
        far_gate = [far(g) for g in grad_gate]
        near_gate = [near(g) for g in grad_gate]

        last_grad = sum(
            jnp.concatenate(
                [dot_tn(normed[slot], grad_value[slot]), dot_tn(upstream_low[slot], hidden[slot])],
                axis=1,
            )
            for slot in range(slots)
        )
        last_sum = Halving(row_blocks(last_grad)).launch(1)

        first = core == 0
        branches = [dot_nt(hidden[slot], out_all) for slot in range(slots)]
        branch_keep = jnp.where(first, branches[0], branches[1])
        branch_give = jnp.where(first, branches[1], branches[0]).astype(BF)

        def mix_blocks(pieces):
            size = hidden_width // parts_of
            blocks = []
            for quarter in pieces:
                g = sum(dot_tn(both[slot], after(quarter[slot], last_sum.give)) for slot in range(slots))
                blocks += [g[:, i * size : (i + 1) * size] for i in range(parts_of)]
            return blocks

        low_masks = [1 << i for i in range(parts_of.bit_length() - 1)]

        def finish_low(halving, *anchors):
            for mask in low_masks[1:]:
                halving.land(*anchors).launch(mask)
            return halving.land(*anchors).launch(parts_of, core == 1)

        def start_low(blocks):
            halving = Halving(blocks)
            return halving.launch(low_masks[0]) if low_masks else halving

        near_sum = start_low(mix_blocks([grad_gate, near_gate]))
        branch_pair = (branch_keep + near(branch_give).astype(F32)).astype(BF)

        early = jnp.concatenate(
            [sum(g[0:1] for g in gate_sums), sum(g[1:2] for g in gate_sums), sum(p[5] for p in pre)], axis=0
        )
        early = total_over_dp(early)

        def back(slot, arrived, lag, *anchors):
            pieces = [grad_gate[slot], near_gate[slot], arrived, near(arrived)]
            pieces[0] = after(pieces[0], *anchors)
            return pieces[3], conv_backward(
                pieces,
                mix_of,
                spectra,
                u[slot],
                slope[slot],
                low[slot],
                state_skip,
                fourier_rows,
                fourier_cols,
                lag,
            )

        def features(slot, grad_feed):
            v = dot_nt(grad_value[slot], value_full) + dot_nt(grad_feed, feed_full)
            give = lax.dynamic_slice_in_dim(v, (1 - core) * half, half, 0).astype(BF)
            keep = lax.dynamic_slice_in_dim(v, core * half, half, 0)
            return give, keep

        far_near_a, (grad_feed_a, lag, skips_a) = back(
            0, far_gate[0], None, near_sum.give, last_sum.give, branch_pair
        )
        give_a, keep_a = features(0, grad_feed_a)
        near_a = near(give_a)
        last_sum.land(grad_feed_a).launch(2)
        near_sum = finish_low(near_sum, grad_feed_a)

        arrived_b = after(far_gate[1], last_sum.give, near_sum.give, give_a)
        far_near_b = near(arrived_b)
        far_sum = start_low(mix_blocks([[far_gate[0], arrived_b], [far_near_a, far_near_b]]))
        pair_a = (keep_a + near_a.astype(F32)).astype(BF)
        far_near_b, (grad_feed_b, lag, skips_b) = back(1, arrived_b, lag, far_sum.give, pair_a)
        far_a = far(pair_a)
        last_sum.land(grad_feed_b)
        mask = 4
        while mask < dp_size:
            last_sum.launch(mask)
            mask *= 2
            if mask < dp_size:
                last_sum.land(grad_feed_b)
        give_b, keep_b = features(1, grad_feed_b)
        near_b = near(give_b)
        near_sum.land(grad_feed_b)
        far_sum = finish_low(far_sum, give_b)

        feed_sum = Halving(
            row_blocks(dot_tn(normed[0], grad_feed_a) + dot_tn(normed[1], grad_feed_b))
        ).launch(1)
        grad_response = response_grad(after(lag, give_b, far_sum.give), fourier_cols, turn)
        pair_b = (keep_b + after(near_b, grad_response).astype(F32)).astype(BF)
        far_b = far(pair_b)
        far_sum.land(grad_response)
        mix_sum = Halving([near_sum.blocks[0], far_sum.blocks[0]]).launch(2 * parts_of, me >= 2)

        def state_sums(c, *anchors):
            grad_delta, grad_rate, grad_readout = state_grad(
                delta, rate, readout, after(grad_response, *anchors), c
            )
            at = slice(c * channels, (c + 1) * channels)
            grad_skip = skips_a[:, at] + skips_b[:, at]
            return jnp.concatenate([grad_rate[0], grad_readout[0], grad_delta[0], grad_skip], axis=0)

        state_a = state_sums(0, pair_b, mix_sum.give, feed_sum.give)
        mask = 2
        feed_sum.land(state_a)
        while mask < dp_size:
            feed_sum.launch(mask)
            mask *= 2
            if mask < dp_size:
                feed_sum.land()
        state_b = state_sums(1, state_a, feed_sum.give)

        rows = jnp.where(first, inputs[0], inputs[1]).astype(F32)
        live = (time_at < jnp.where(first, lengths[0], lengths[1])).astype(F32)
        branch_far = after(far(branch_pair), pair_b)
        mine = (live * (rows + (branch_pair.astype(F32) + branch_far.astype(F32)) + out_bias)).astype(BF)
        theirs = near(mine)
        layer_out = jnp.stack([jnp.where(first, mine, theirs), jnp.where(first, theirs, mine)])

        input_rows = []
        small = None
        for slot, pair, arrived in ((0, pair_a, after(far_a, state_a)), (1, pair_b, after(far_b, state_b))):
            total = pair.astype(F32) + arrived.astype(F32)
            rows = lax.dynamic_slice_in_dim(inputs[slot], core * half, half, 0).astype(F32)
            up_half = lax.dynamic_slice_in_dim(upstream_low[slot], core * half, half, 0).astype(F32)
            center = rows - jnp.mean(rows, axis=-1, keepdims=True)
            spread = jnp.mean(center * center, axis=-1, keepdims=True)
            inverse = lax.rsqrt(spread + EPSILON)
            unit = center * inverse
            weighted = total * norm_gain
            mine = (
                up_half
                + (
                    weighted
                    - jnp.mean(weighted, axis=-1, keepdims=True)
                    - unit * jnp.mean(weighted * unit, axis=-1, keepdims=True)
                )
                * inverse
            ).astype(BF)
            theirs = near(mine)
            input_rows.append(
                jnp.concatenate(
                    [jnp.where(core == 0, mine, theirs), jnp.where(core == 0, theirs, mine)], axis=0
                )
            )
            now = jnp.concatenate(
                [jnp.sum(total * unit, axis=0, keepdims=True), jnp.sum(total, axis=0, keepdims=True)], axis=0
            )
            small = now if slot == 0 else small + now

        feed_bias_sum = jnp.sum(grad_feed_a.astype(F32), axis=0, keepdims=True) + jnp.sum(
            grad_feed_b.astype(F32), axis=0, keepdims=True
        )
        last_sum = last_sum.land(state_a).blocks[0]
        feed_sum = feed_sum.land(state_b).blocks[0]
        mix_sum = mix_sum.land(state_b).blocks[0]
        totals = [total_over_dp(state_a), total_over_dp(state_b)]
        feed_bias_sum = total_over_dp(feed_bias_sum)
        small = total_over_dp(small)
        norm_sums = small + near(small)
        last_rows = jnp.stack([v[2 * states :] for v in totals])

        return (
            layer_out,
            jnp.stack(input_rows),
            norm_sums[0],
            norm_sums[1],
            last_sum[:, :hidden_width],
            early[1],
            feed_sum,
            feed_bias_sum[0],
            mix_sum[:channels],
            mix_sum[channels:],
            early[0],
            last_sum[:, hidden_width:].T,
            early[2],
            last_rows[:, 0],
            jnp.swapaxes(jnp.stack([v[:states] for v in totals]), 1, 2),
            jnp.swapaxes(jnp.stack([v[states : 2 * states] for v in totals]), 1, 2),
            last_rows[:, 1],
        )

    return shards


def solution(mesh):
    placed = (
        P("dp", None, None),
        P("dp", None, None),
        P("dp"),
        P(),
        P(),
        P("dp", "tensor"),
        P("tensor"),
        P("dp", "tensor"),
        P("tensor"),
        P("tensor", "dp"),
        P("tensor", "dp"),
        P("tensor"),
        P("tensor", "dp"),
        P(),
        P(None, "tensor"),
        P(None, "tensor", None),
        P(None, "tensor", None),
        P(None, "tensor"),
    )
    return jax.shard_map(
        make_shards(mesh.shape["dp"], mesh.shape["tensor"]),
        mesh=mesh,
        in_specs=placed,
        out_specs=(
            P("dp", None, None),
            P("dp", None, None),
            P(),
            P(),
            P("dp", "tensor"),
            P("tensor"),
            P("dp", "tensor"),
            P("tensor"),
            P("tensor", "dp"),
            P("tensor", "dp"),
            P("tensor"),
            P("tensor", "dp"),
            P(),
            P(None, "tensor"),
            P(None, "tensor", None),
            P(None, "tensor", None),
            P(None, "tensor"),
        ),
        check_vma=False,
    )
```

time: 781 us -> 544 us (0.70)
  waiting for transfers between devices: 276 us -> 62 us
  Pallas kernels: 73.1 us -> 242 us
  matrix products: 165 us -> 52.1 us
  other arithmetic: 133 us -> 83.2 us
  blocking collectives: 37.1 us -> 0 us
  starting transfers between devices: 13.4 us -> 46.2 us
  local copies, waits for them, and re-layouts: 56.9 us -> 30.1 us
    pallas_call x2 -> x18, Pallas kernels: 73.1 us -> 242 us  [the longest x2 50.1 us: conv_backward(): pl.pallas_call(kernel, name='conv_backward', grid=(bands,), in_specs=[who...]
    ppermute x8 -> x7, waiting for transfers between devices: 104 us -> 9.9 us  [far(): return lax.ppermute(v, 'tensor', far_swap)]
    reduce_scatter x2 -> x0, waiting for transfers between devices: 84.7 us -> none  [the longest x1 62.5 us: shards(): lax.psum_scatter(grad_feed_w.astype(BF), 'dp', scatter_dimension=0, tiled...]
    unnamed x8 -> x2, waiting for transfers between devices: 71.3 us -> 0.03 us
    dot_general x19 -> x0, matrix products: 62.8 us -> none  [dot_nn(): return jnp.dot(a, b, preferred_element_type=F32)]
    ppermute x0 -> x29, waiting for transfers between devices: none -> 52 us  [across(): return lax.ppermute(v, 'dp', [(i, i ^ mask) for i in range(dp_size)])]
    psum x1 -> x0, blocking collectives: 37.1 us -> none  [shards(): sums = lax.psum(flat, 'dp')]
    ppermute x0 -> x29, starting transfers between devices: none -> 36 us  [across(): return lax.ppermute(v, 'dp', [(i, i ^ mask) for i in range(dp_size)])]
  transfers between devices with their start and end apart: 30 -> 53, of which waited for: 8 -> 17; matrix products, arithmetic and copies ran while one was open for 42% -> 28% of each run, Pallas kernels for 9% -> 43%
where the time goes in v2:
time: 544 us; the launch traced here: 533 us
  Pallas kernels  242 us (44%)
  other arithmetic  83.2 us (15%)
  waiting for transfers between devices  62 us (11%)
  matrix products  52.1 us (10%)
  starting transfers between devices  46.2 us (8%)
  local copies, waits for them, and re-layouts  30.1 us (6%)
  between operations  17.2 us (3%)
    ppermute x29, waiting for transfers between devices, across(): return lax.ppermute(v, 'dp', [(i, i ^ mask) for i in range(dp_size)])  52 us
    pallas_call x2, Pallas kernels, conv_backward(): pl.pallas_call(kernel, name='conv_backward', grid=(bands,), in_specs=[who...  50.1 us
    pallas_call x2, Pallas kernels, impulse(): pl.pallas_call(impulse_kernel, name='impulse', grid=(lanes,), in_specs=[p...  39.9 us
    pallas_call x2, Pallas kernels, state_grad(): pl.pallas_call(state_grad_kernel, name='state_grad', grid=(lanes,), in_sp...  36.7 us
    ppermute x29, starting transfers between devices, across(): return lax.ppermute(v, 'dp', [(i, i ^ mask) for i in range(dp_size)])  36 us
    dot_general x14, matrix products, dot_tn(): lax.dot_general(a, b, (((0,), (0,)), ((), ())), preferred_element_type=F32)  35.9 us
    pallas_call x2, Pallas kernels, conv_forward(): pl.pallas_call(functools.partial(conv_forward_kernel, slot), name='conv_f...  32.8 us
    pallas_call x2, Pallas kernels, before_gate(): pl.pallas_call(functools.partial(before_gate_kernel, slot), name='before_...  23.9 us
  transfers between devices with their start and end apart: 53, of which 17 were waited for; matrix products, arithmetic and copies ran while one was open for 28% of the time, Pallas kernels for 43%

profile of v2, /device:TPU:0, one launch (start us, length us, event | category | flops | bytes accessed | tf_op | source)
XLA Modules:
  0.0 533.4 jit_solution(17684908181091090724)
XLA Ops:
  9.4 4.1 collective-permute-start
  21.4 5.9 %collective-permute-done.1 = bf16[2,96,384]{2,1,0:T(8,128)(2,1)S(1)} collective-permute-done((bf16[2,96,384]{2,1,0:T(8,128)(2,1)S(1)}, bf16[2,96,384]{2,1,0:T(8,128)(2,1)S(1)}, u32[]{:S(2)}, u32[]{:S(2)}) %collective-permute-start.1) | collective-permute-done | bytes 147488 | tf_op jit(solution)/shard_map/ppermute | solution.py:546
  31.2 19.9 %impulse.2.first_ref = bf16[1024,384]{1,0:T(8,128)(2,1)} custom-call(f32[2,1,384]{2,1,0:T(1,128)} %broadcast_in_dim.20.delta_ref, f32[2,64,384]{2,1,0:T(8,128)} %bitcast.221, f32[2,64,384]{2,1,0:T(8,128)} %bitcast.225), custom_call_target="tpu_custom_call" | custom-call | tf_op jit(solution)/shard_map/impulse/pallas_call | solution.py:92
  51.2 20.0 %impulse.3.second_ref = bf16[1024,384]{1,0:T(8,128)(2,1)} custom-call(f32[2,1,384]{2,1,0:T(1,128)} %broadcast_in_dim.20.delta_ref, f32[2,64,384]{2,1,0:T(8,128)} %bitcast.222, f32[2,64,384]{2,1,0:T(8,128)} %bitcast.226), custom_call_target="tpu_custom_call" | custom-call | tf_op jit(solution)/shard_map/impulse/pallas_call | solution.py:92
  71.1 8.7 %response.1.k_ref.refs_10_ = f32[4,2,256,768]{3,2,1,0:T(8,128)} custom-call(bf16[1024,384]{1,0:T(8,128)(2,1)} %impulse.2.first_ref, bf16[1024,384]{1,0:T(8,128)(2,1)} %impulse.3.second_ref, bf16[2048,1024]{1,0:T(8,128)(2,1)} %constant.70.clone.rows_ref.refs_8_, f32[2,1024,128]{2,1,0:T(8,128)} %constant.72.clone.turn_ref), custom_call_target="tpu_custom_call" | custom-call | tf_op jit(solution)/shard_map/response/pallas_call | solution.py:205
  81.8 16.4 %conv_forward.2 = (f32[1024,384]{1,0:T(8,128)}, bf16[1024,384]{1,0:T(8,128)(2,1)}, f32[2048,384]{1,0:T(8,128)}, bf16[1024,768]{1,0:T(8,128)(2,1)}) custom-call(s32[2]{0:T(128)} %length_ref.7, bf16[1024,768]{1,0:T(8,128)(2,1)} %get-tuple-element.274.normed_ref, bf16[768,384]{1,0:T(8,128)(2,1)} %bitcast.216, f32[1,384]{1,0:T(1,128)} %broadcast_in_dim.19.bias_ref, ...), custom_call_target="tpu_custom_call" | custom-call | tf_op jit(solution)/shard_map/conv_forward/pallas_call | solution.py:425
  98.2 4.0 dynamic-slice_bitcast_fusion.3
  103.9 6.0 %send.2 = (bf16[1024,768]{1,0:T(8,128)(2,1)}, bf16[1024,768]{1,0:T(8,128)(2,1)}) custom-call(bf16[1024,768]{1,0:T(8,128)(2,1)} %get-tuple-element.97.a_ref.both_ref, bf16[768,768]{1,0:T(8,128)(2,1)} %get-tuple-element.323.first_ref.refs_5_, bf16[768,768]{1,0:T(8,128)(2,1)} %get-tuple-element.324.second_ref.refs_7_), custom_call_target="tpu_custom_call" | custom-call | tf_op jit(solution)/shard_map/send/pallas_call | solution.py:264
  109.9 16.4 %conv_forward.3 = (f32[1024,384]{1,0:T(8,128)}, bf16[1024,384]{1,0:T(8,128)(2,1)}, f32[2048,384]{1,0:T(8,128)}, bf16[1024,768]{1,0:T(8,128)(2,1)}) custom-call(s32[2]{0:T(128)} %length_ref.7, bf16[1024,768]{1,0:T(8,128)(2,1)} %get-tuple-element.275.normed_ref, bf16[768,384]{1,0:T(8,128)(2,1)} %bitcast.217, f32[1,384]{1,0:T(1,128)} %broadcast_in_dim.19.bias_ref, ...), custom_call_target="tpu_custom_call" | custom-call | tf_op jit(solution)/shard_map/conv_forward/pallas_call | solution.py:425
  127.5 5.2 join.2
  132.7 6.1 %send.3 = (bf16[1024,768]{1,0:T(8,128)(2,1)}, bf16[1024,768]{1,0:T(8,128)(2,1)}) custom-call(bf16[1024,768]{1,0:T(8,128)(2,1)} %get-tuple-element.101.a_ref.both_ref, bf16[768,768]{1,0:T(8,128)(2,1)} %get-tuple-element.323.first_ref.refs_5_, bf16[768,768]{1,0:T(8,128)(2,1)} %get-tuple-element.324.second_ref.refs_7_), custom_call_target="tpu_custom_call" | custom-call | tf_op jit(solution)/shard_map/send/pallas_call | solution.py:264
  149.9 5.4 %join.3 = bf16[1024,768]{1,0:T(8,128)(2,1)} custom-call(bf16[1024,768]{1,0:T(8,128)(2,1)} %get-tuple-element.101.a_ref.both_ref, bf16[768,768]{1,0:T(8,128)(2,1)} %pad_maximum_fusion.5.b_ref.refs_6_, bf16[1024,768]{1,0:T(8,128)(2,1)} %collective-permute-done.5.add_ref), custom_call_target="tpu_custom_call" | custom-call | tf_op jit(solution)/shard_map/join/pallas_call | solution.py:281
  158.2 12.0 %before_gate.3 = (f32[1024,768]{1,0:T(8,128)}, f32[1024,768]{1,0:T(8,128)}, f32[1024,768]{1,0:T(8,128)}, f32[1024,768]{1,0:T(8,128)}, bf16[1024,768]{1,0:T(8,128)(2,1)}, /*index=5*/f32[1,768]{1,0:T(1,128)}) custom-call(s32[2]{0:T(128)} %length_ref.7, bf16[1024,768]{1,0:T(8,128)(2,1)} %get-tuple-element.101.a_ref.both_ref, ...), custom_call_target="tpu_custom_call" | custom-call | tf_op jit(solution)/shard_map/before_gate/pallas_call | solution.py:318
  170.2 9.9 %collective-permute-done.6.far_ref = bf16[1024,768]{1,0:T(8,128)(2,1)} collective-permute-done((bf16[1024,768]{1,0:T(8,128)(2,1)}, bf16[1024,768]{1,0:T(8,128)(2,1)}, u32[]{:S(2)}, u32[]{:S(2)}) %collective-permute-start.6) | collective-permute-done | bytes 1572896 | tf_op jit(solution)/shard_map/ppermute | solution.py:543
  180.0 11.9 %before_gate.2 = (f32[1024,768]{1,0:T(8,128)}, f32[1024,768]{1,0:T(8,128)}, f32[1024,768]{1,0:T(8,128)}, f32[1024,768]{1,0:T(8,128)}, bf16[1024,768]{1,0:T(8,128)(2,1)}, /*index=5*/f32[1,768]{1,0:T(1,128)}) custom-call(s32[2]{0:T(128)} %length_ref.7, bf16[1024,768]{1,0:T(8,128)(2,1)} %get-tuple-element.97.a_ref.both_ref, ...), custom_call_target="tpu_custom_call" | custom-call | tf_op jit(solution)/shard_map/before_gate/pallas_call | solution.py:318
  191.9 8.6 %gate.2 = (bf16[1024,768]{1,0:T(8,128)(2,1)}, bf16[1024,768]{1,0:T(8,128)(2,1)}, bf16[1024,768]{1,0:T(8,128)(2,1)}, f32[2,768]{1,0:T(2,128)}) custom-call(f32[1024,768]{1,0:T(8,128)} %get-tuple-element.104.part_ref, bf16[1024,768]{1,0:T(8,128)(2,1)} %collective-permute-done.6.far_ref, f32[1024,768]{1,0:T(8,128)} %get-tuple-element.108.act_ref, ...), custom_call_target="tpu_custom_call" | custom-call | tf_op jit(solution)/shard_map/gate/pallas_call | solution.py:361
  202.2 4.6 fusion.54
  215.7 9.0 %gate.3 = (bf16[1024,768]{1,0:T(8,128)(2,1)}, bf16[1024,768]{1,0:T(8,128)(2,1)}, bf16[1024,768]{1,0:T(8,128)(2,1)}, f32[2,768]{1,0:T(2,128)}) custom-call(f32[1024,768]{1,0:T(8,128)} %get-tuple-element.106.part_ref, bf16[1024,768]{1,0:T(8,128)(2,1)} %collective-permute-done.8.far_ref, f32[1024,768]{1,0:T(8,128)} %get-tuple-element.114.act_ref, ...), custom_call_target="tpu_custom_call" | custom-call | tf_op jit(solution)/shard_map/gate/pallas_call | solution.py:361
  224.7 4.5 fusion.66
  266.3 24.2 %conv_backward.2 = (bf16[1024,384]{1,0:T(8,128)(2,1)}, f32[2048,768]{1,0:T(8,128)}, f32[1,768]{1,0:T(1,128)}) custom-call(bf16[1024,768]{1,0:T(8,128)(2,1)} %get-tuple-element.127.refs_0_, bf16[1024,768]{1,0:T(8,128)(2,1)} %collective-permute-done.13.refs_1_, bf16[1024,768]{1,0:T(8,128)(2,1)} %collective-permute-done.11.refs_2_, ...), custom_call_target="tpu_custom_call" | custom-call | tf_op jit(solution)/shard_map/conv_backward/pallas_call | solution.py:512
  295.2 5.0 select_convert_fusion.10
  322.2 3.6 fusion.71
  329.9 26.0 %conv_backward.3 = (bf16[1024,384]{1,0:T(8,128)(2,1)}, f32[2048,768]{1,0:T(8,128)}, f32[1,768]{1,0:T(1,128)}) custom-call(bf16[1024,768]{1,0:T(8,128)(2,1)} %get-tuple-element.139.refs_0_, bf16[1024,768]{1,0:T(8,128)(2,1)} %copy-done.51, bf16[1024,768]{1,0:T(8,128)(2,1)} %collective-permute-done.16.refs_2_, ...), custom_call_target="tpu_custom_call" | custom-call | tf_op jit(solution)/shard_map/conv_backward/pallas_call | solution.py:512
  385.6 10.1 %response_grad.1.grad_ref = f32[1024,768]{1,0:T(8,128)} custom-call(f32[2048,768]{1,0:T(8,128)} %get-tuple-element.147.lag_ref, bf16[1024,2048]{1,0:T(8,128)(2,1)} %constant.71.clone.cols_ref.refs_9_, f32[2,1024,128]{2,1,0:T(8,128)} %constant.72.clone.turn_ref), custom_call_target="tpu_custom_call" | custom-call | tf_op jit(solution)/shard_map/response_grad/pallas_call | solution.py:241
  400.5 3.6 fusion.16
  404.1 7.3 %collective-permute-done.25 = bf16[768,384]{1,0:T(8,128)(2,1)S(1)} collective-permute-done((bf16[768,384]{1,0:T(8,128)(2,1)S(1)}, bf16[768,384]{1,0:T(8,128)(2,1)S(1)}, u32[]{:S(2)}, u32[]{:S(2)}) %collective-permute-start.25) | collective-permute-done | bytes 589856 | tf_op jit(solution)/shard_map/ppermute | solution.py:546
  414.5 18.5 %state_grad.2 = (f32[1,1,384]{2,1,0:T(1,128)}, f32[1,64,384]{2,1,0:T(8,128)}, f32[1,64,384]{2,1,0:T(8,128)}) custom-call(f32[2,1,384]{2,1,0:T(1,128)} %broadcast_in_dim.20.delta_ref, f32[2,64,384]{2,1,0:T(8,128)} %bitcast.223, f32[2,64,384]{2,1,0:T(8,128)} %bitcast.227, f32[1024,768]{1,0:T(8,128)} %response_grad.1.grad_ref), custom_call_target="tpu_custom_call" | custom-call | tf_op jit(solution)/shard_map/state_grad/pallas_call | solution.py:156
  446.1 18.3 %state_grad.3 = (f32[1,1,384]{2,1,0:T(1,128)}, f32[1,64,384]{2,1,0:T(8,128)}, f32[1,64,384]{2,1,0:T(8,128)}) custom-call(f32[2,1,384]{2,1,0:T(1,128)} %broadcast_in_dim.20.delta_ref, f32[2,64,384]{2,1,0:T(8,128)} %bitcast.224, f32[2,64,384]{2,1,0:T(8,128)} %bitcast.228, f32[1024,768]{1,0:T(8,128)} %response_grad.1.grad_ref), custom_call_target="tpu_custom_call" | custom-call | tf_op jit(solution)/shard_map/state_grad/pallas_call | solution.py:156
  473.4 3.6 collective-permute-done.32
  491.6 3.4 collective-permute-done.46
  503.2 9.7 %collective-permute-done.47 = f32[130,384]{1,0:T(8,128)S(1)} collective-permute-done((f32[130,384]{1,0:T(8,128)S(1)}, f32[130,384]{1,0:T(8,128)S(1)}, u32[]{:S(2)}, u32[]{:S(2)}) %collective-permute-start.47) | collective-permute-done | bytes 199712 | tf_op jit(solution)/shard_map/ppermute | solution.py:546
  512.9 4.1 collective-permute-done.50
  (424 shorter events, 200.4 us)
Async XLA Ops:
  7.2 91.0 %all-gather.6.cloned.1.call-start = ((), (), s32[]{:S(2)}) async-start(), calls=%async_computation.1 | async-start | bytes 5308416 | tf_op jit(solution)/shard_map/all_gather | solution.py:628
  9.3 148.8 %all-gather.4.cloned.1.call-start = ((), (), s32[]{:S(2)}) async-start(), calls=%async_computation | async-start | bytes 2654208 | tf_op jit(solution)/shard_map/all_gather | solution.py:630
  27.4 52.4 %collective-permute-start.2 = (bf16[4,96,384]{2,1,0:T(8,128)(2,1)S(1)}, bf16[4,96,384]{2,1,0:T(8,128)(2,1)}, u32[]{:S(2)}, u32[]{:S(2)}) collective-permute-start(bf16[4,96,384]{2,1,0:T(8,128)(2,1)S(1)} %bitcast.229), channel_id=1, source_target_pairs={{0,4},{4,0},{8,12},{12,8},{16,20},{20,16},{24,28},{28,24},{1,5},{5... | collective-permute-start | bytes 884744 | tf_op jit(solution)/shard_map/ppermute | solution.py:546
  109.9 17.6 %collective-permute-start.4 = (bf16[1024,768]{1,0:T(8,128)(2,1)}, bf16[1024,768]{1,0:T(8,128)(2,1)}, u32[]{:S(2)}, u32[]{:S(2)}) collective-permute-start(bf16[1024,768]{1,0:T(8,128)(2,1)} %get-tuple-element.100), channel_id=1, source_target_pairs={{0,1},{1,0},{2,3},{3,2},{4,5},{5,4},{6,7},{7,6},{8,9},{9,8},{10,11... | collective-permute-start | bytes 4718600 | tf_op jit(solution)/shard_map/ppermute | solution.py:540
  142.4 37.6 %collective-permute-start.3 = (bf16[1024,768]{1,0:T(8,128)(2,1)}, bf16[1024,768]{1,0:T(8,128)(2,1)}, u32[]{:S(2)}, u32[]{:S(2)}) collective-permute-start(bf16[1024,768]{1,0:T(8,128)(2,1)} %get-tuple-element.98), channel_id=1, source_target_pairs={{0,1},{1,0},{2,3},{3,2},{4,5},{5,4},{6,7},{7,6},{8,9},{9,8},{10,11... | collective-permute-start | bytes 4718600 | tf_op jit(solution)/shard_map/ppermute | solution.py:540
  142.5 37.6 %collective-permute-start.6 = (bf16[1024,768]{1,0:T(8,128)(2,1)}, bf16[1024,768]{1,0:T(8,128)(2,1)}, u32[]{:S(2)}, u32[]{:S(2)}) collective-permute-start(bf16[1024,768]{1,0:T(8,128)(2,1)} %join.2), channel_id=1, source_target_pairs={{0,2},{1,3},{2,0},{3,1},{4,6},{5,7},{6,4},{7,5},{8,10},{9,11},{10,... | collective-permute-start | bytes 4718600 | tf_op jit(solution)/shard_map/ppermute | solution.py:543
  155.3 60.4 %collective-permute-start.8 = (bf16[1024,768]{1,0:T(8,128)(2,1)}, bf16[1024,768]{1,0:T(8,128)(2,1)}, u32[]{:S(2)}, u32[]{:S(2)}) collective-permute-start(bf16[1024,768]{1,0:T(8,128)(2,1)} %join.3), channel_id=1, source_target_pairs={{0,2},{1,3},{2,0},{3,1},{4,6},{5,7},{6,4},{7,5},{8,10},{9,11},{10,... | collective-permute-start | bytes 4718600 | tf_op jit(solution)/shard_map/ppermute | solution.py:543
  200.5 50.5 %collective-permute-start.13 = (bf16[1024,768]{1,0:T(8,128)(2,1)}, bf16[1024,768]{1,0:T(8,128)(2,1)}, u32[]{:S(2)}, u32[]{:S(2)}) collective-permute-start(bf16[1024,768]{1,0:T(8,128)(2,1)} %get-tuple-element.127.refs_0_), channel_id=1, source_target_pairs={{0,1},{1,0},{2,3},{3,2},{4,5},{5,4},{6,7},{7,6},{8,9},{9,8},{10,11... | collective-permute-start | bytes 4718600 | tf_op jit(solution)/shard_map/ppermute | solution.py:540
  200.5 50.9 %collective-permute-start.11 = (bf16[1024,768]{1,0:T(8,128)(2,1)}, bf16[1024,768]{1,0:T(8,128)(2,1)}, u32[]{:S(2)}, u32[]{:S(2)}) collective-permute-start(bf16[1024,768]{1,0:T(8,128)(2,1)} %get-tuple-element.127.refs_0_), channel_id=1, source_target_pairs={{0,2},{1,3},{2,0},{3,1},{4,6},{5,7},{6,4},{7,5},{8,10},{9,11},{10,... | collective-permute-start | bytes 4718600 | tf_op jit(solution)/shard_map/ppermute | solution.py:543
  239.6 15.9 %collective-permute-start.14 = (bf16[1024,768]{1,0:T(8,128)(2,1)}, bf16[1024,768]{1,0:T(8,128)(2,1)S(1)}, u32[]{:S(2)}, u32[]{:S(2)}) collective-permute-start(bf16[1024,768]{1,0:T(8,128)(2,1)} %get-tuple-element.139.refs_0_), channel_id=1, source_target_pairs={{0,1},{1,0},{2,3},{3,2},{4,5},{5,4},{6,7},{7,6},{8,9},{9,8},{10,11... | collective-permute-start | bytes 4718600 | tf_op jit(solution)/shard_map/ppermute | solution.py:540
  243.3 20.0 %collective-permute-start.9 = (bf16[1024,768]{1,0:T(8,128)(2,1)S(1)}, bf16[1024,768]{1,0:T(8,128)(2,1)S(1)}, u32[]{:S(2)}, u32[]{:S(2)}) collective-permute-start(bf16[1024,768]{1,0:T(8,128)(2,1)S(1)} %get-tuple-element.319), channel_id=1, source_target_pairs={{0,1},{1,0},{2,3},{3,2},{4,5},{5,4},{6,7},{7,6},{8,9},{9,8},{10,11... | collective-permute-start | bytes 4718600 | tf_op jit(solution)/shard_map/ppermute | solution.py:540
  251.0 44.2 %collective-permute-start.12 = (bf16[384,1536]{0,1:T(8,128)(2,1)}, bf16[384,1536]{0,1:T(8,128)(2,1)}, u32[]{:S(2)}, u32[]{:S(2)}) collective-permute-start(bf16[384,1536]{0,1:T(8,128)(2,1)} %pad_maximum_fusion.6), channel_id=1, source_target_pairs={{0,4},{4,0},{8,12},{12,8},{16,20},{20,16},{24,28},{28,24},{1,5},{5... | collective-permute-start | bytes 3538952 | tf_op jit(solution)/shard_map/ppermute | solution.py:546
  251.4 55.4 %collective-permute-start.16 = (bf16[1024,768]{1,0:T(8,128)(2,1)}, bf16[1024,768]{1,0:T(8,128)(2,1)}, u32[]{:S(2)}, u32[]{:S(2)}) collective-permute-start(bf16[1024,768]{1,0:T(8,128)(2,1)} %get-tuple-element.139.refs_0_), channel_id=1, source_target_pairs={{0,2},{1,3},{2,0},{3,1},{4,6},{5,7},{6,4},{7,5},{8,10},{9,11},{10,... | collective-permute-start | bytes 4718600 | tf_op jit(solution)/shard_map/ppermute | solution.py:543
  263.0 40.8 %collective-permute-start.17 = (bf16[1536,384]{1,0:T(8,128)(2,1)}, bf16[1536,384]{1,0:T(8,128)(2,1)}, u32[]{:S(2)}, u32[]{:S(2)}) collective-permute-start(bf16[1536,384]{1,0:T(8,128)(2,1)} %pad_maximum_fusion.7), channel_id=1, source_target_pairs={{0,4},{4,0},{8,12},{12,8},{16,20},{20,16},{24,28},{28,24},{1,5},{5... | collective-permute-start | bytes 3538952 | tf_op jit(solution)/shard_map/ppermute | solution.py:546
  295.0 16.8 %collective-permute-start.19 = (bf16[512,768]{1,0:T(8,128)(2,1)}, bf16[512,768]{1,0:T(8,128)(2,1)}, u32[]{:S(2)}, u32[]{:S(2)}) collective-permute-start(bf16[512,768]{1,0:T(8,128)(2,1)} %dynamic-slice_convert_fusion.1), channel_id=1, source_target_pairs={{0,1},{1,0},{2,3},{3,2},{4,5},{5,4},{6,7},{7,6},{8,9},{9,8},{10,11... | collective-permute-start | bytes 2359304 | tf_op jit(solution)/shard_map/ppermute | solution.py:540
  309.7 89.2 %collective-permute-start.10 = (bf16[1024,768]{1,0:T(8,128)(2,1)}, bf16[1024,768]{1,0:T(8,128)(2,1)}, u32[]{:S(2)}, u32[]{:S(2)}) collective-permute-start(bf16[1024,768]{1,0:T(8,128)(2,1)} %add_convert_fusion), channel_id=1, source_target_pairs={{0,2},{1,3},{2,0},{3,1},{4,6},{5,7},{6,4},{7,5},{8,10},{9,11},{10,... | collective-permute-start | bytes 4718600 | tf_op jit(solution)/shard_map/ppermute | solution.py:543
  310.1 54.1 %collective-permute-start.35 = (bf16[192,1536]{1,0:T(8,128)(2,1)}, bf16[192,1536]{1,0:T(8,128)(2,1)}, u32[]{:S(2)}, u32[]{:S(2)}) collective-permute-start(bf16[192,1536]{1,0:T(8,128)(2,1)} %copy.47), channel_id=1, source_target_pairs={{0,8},{4,12},{8,0},{12,4},{16,24},{20,28},{24,16},{28,20},{1,9},{5... | collective-permute-start | bytes 1769480 | tf_op jit(solution)/shard_map/ppermute | solution.py:546
  314.6 63.6 %collective-permute-start.24 = (bf16[768,384]{1,0:T(8,128)(2,1)}, bf16[768,384]{1,0:T(8,128)(2,1)}, u32[]{:S(2)}, u32[]{:S(2)}) collective-permute-start(bf16[768,384]{1,0:T(8,128)(2,1)} %get-tuple-element.250), channel_id=1, source_target_pairs={{0,8},{4,12},{8,0},{12,4},{16,24},{20,28},{24,16},{28,20},{1,9},{5... | collective-permute-start | bytes 1769480 | tf_op jit(solution)/shard_map/ppermute | solution.py:546
  329.1 52.2 %collective-permute-start.21 = (bf16[1536,384]{1,0:T(8,128)(2,1)}, bf16[1536,384]{1,0:T(8,128)(2,1)}, u32[]{:S(2)}, u32[]{:S(2)}) collective-permute-start(bf16[1536,384]{1,0:T(8,128)(2,1)} %pad_maximum_fusion.8), channel_id=1, source_target_pairs={{0,4},{4,0},{8,12},{12,8},{16,20},{20,16},{24,28},{28,24},{1,5},{5... | collective-permute-start | bytes 3538952 | tf_op jit(solution)/shard_map/ppermute | solution.py:546
  360.6 35.0 %collective-permute-start.20 = (bf16[512,768]{1,0:T(8,128)(2,1)}, bf16[512,768]{1,0:T(8,128)(2,1)}, u32[]{:S(2)}, u32[]{:S(2)}) collective-permute-start(bf16[512,768]{1,0:T(8,128)(2,1)} %dynamic-slice_convert_fusion), channel_id=1, source_target_pairs={{0,1},{1,0},{2,3},{3,2},{4,5},{5,4},{6,7},{7,6},{8,9},{9,8},{10,11... | collective-permute-start | bytes 2359304 | tf_op jit(solution)/shard_map/ppermute | solution.py:540
  378.2 64.2 %collective-permute-start.23 = (bf16[512,768]{1,0:T(8,128)(2,1)}, bf16[512,768]{1,0:T(8,128)(2,1)}, u32[]{:S(2)}, u32[]{:S(2)}) collective-permute-start(bf16[512,768]{1,0:T(8,128)(2,1)} %add_convert_fusion.2), channel_id=1, source_target_pairs={{0,2},{1,3},{2,0},{3,1},{4,6},{5,7},{6,4},{7,5},{8,10},{9,11},{10,... | collective-permute-start | bytes 2359304 | tf_op jit(solution)/shard_map/ppermute | solution.py:543
  380.0 54.8 %collective-permute-start.28 = (bf16[384,384]{1,0:T(8,128)(2,1)S(1)}, bf16[384,384]{1,0:T(8,128)(2,1)}, u32[]{:S(2)}, u32[]{:S(2)}) collective-permute-start(bf16[384,384]{1,0:T(8,128)(2,1)S(1)} %pad_maximum_fusion.14), channel_id=1, source_target_pairs={{0,4},{4,0},{8,12},{12,8},{16,20},{20,16},{24,28},{28,24},{1,5},{5... | collective-permute-start | bytes 884744 | tf_op jit(solution)/shard_map/ppermute | solution.py:546
  381.3 57.6 %collective-permute-start.36 = (bf16[96,1536]{0,1:T(8,128)(2,1)}, bf16[96,1536]{0,1:T(8,128)(2,1)}, u32[]{:S(2)}, u32[]{:S(2)}) collective-permute-start(bf16[96,1536]{0,1:T(8,128)(2,1)} %select_convert_fusion.8), channel_id=1, source_target_pairs={{0,16},{4,20},{8,24},{12,28},{16,0},{20,4},{24,8},{28,12},{1,17},{... | collective-permute-start | bytes 884744 | tf_op jit(solution)/shard_map/ppermute | solution.py:546
  395.6 15.7 %collective-permute-start.25 = (bf16[768,384]{1,0:T(8,128)(2,1)S(1)}, bf16[768,384]{1,0:T(8,128)(2,1)S(1)}, u32[]{:S(2)}, u32[]{:S(2)}) collective-permute-start(bf16[768,384]{1,0:T(8,128)(2,1)S(1)} %get-tuple-element.247), channel_id=1, source_target_pairs={{0,8},{4,12},{8,0},{12,4},{16,24},{20,28},{24,16},{28,20},{1,9},{5... | collective-permute-start | bytes 1769480 | tf_op jit(solution)/shard_map/ppermute | solution.py:546
  398.9 67.4 %collective-permute-start.27 = (bf16[512,768]{1,0:T(8,128)(2,1)}, bf16[512,768]{1,0:T(8,128)(2,1)}, u32[]{:S(2)}, u32[]{:S(2)}) collective-permute-start(bf16[512,768]{1,0:T(8,128)(2,1)} %add_convert_fusion.1), channel_id=1, source_target_pairs={{0,2},{1,3},{2,0},{3,1},{4,6},{5,7},{6,4},{7,5},{8,10},{9,11},{10,... | collective-permute-start | bytes 2359304 | tf_op jit(solution)/shard_map/ppermute | solution.py:543
  411.3 110.7 %collective-permute-start.22 = (bf16[1024,768]{1,0:T(8,128)(2,1)}, bf16[1024,768]{1,0:T(8,128)(2,1)}, u32[]{:S(2)}, u32[]{:S(2)}) collective-permute-start(bf16[1024,768]{1,0:T(8,128)(2,1)} %fusion.16), channel_id=1, source_target_pairs={{0,1},{1,0},{2,3},{3,2},{4,5},{5,4},{6,7},{7,6},{8,9},{9,8},{10,11... | collective-permute-start | bytes 4718600 | tf_op jit(solution)/shard_map/ppermute | solution.py:540
  434.7 48.6 %collective-permute-start.45 = (f32[130,384]{1,0:T(8,128)}, f32[130,384]{1,0:T(8,128)}, u32[]{:S(2)}, u32[]{:S(2)}) collective-permute-start(f32[130,384]{1,0:T(8,128)} %pad_maximum_fusion.15), channel_id=1, source_target_pairs={{0,4},{4,0},{8,12},{12,8},{16,20},{20,16},{24,28},{28,24},{1,5},{5... | collective-permute-start | bytes 599048 | tf_op jit(solution)/shard_map/ppermute | solution.py:546
  442.4 56.2 %collective-permute-start.44 = (bf16[768,384]{1,0:T(8,128)(2,1)}, bf16[768,384]{1,0:T(8,128)(2,1)}, u32[]{:S(2)}, u32[]{:S(2)}) collective-permute-start(bf16[768,384]{1,0:T(8,128)(2,1)} %select_convert_fusion.1), channel_id=1, source_target_pairs={{0,16},{4,20},{8,24},{12,28},{16,0},{20,4},{24,8},{28,12},{1,17},{... | collective-permute-start | bytes 1769480 | tf_op jit(solution)/shard_map/ppermute | solution.py:546
  465.4 22.7 %collective-permute-start.48 = (f32[130,384]{1,0:T(8,128)S(1)}, f32[130,384]{1,0:T(8,128)S(1)}, u32[]{:S(2)}, u32[]{:S(2)}) collective-permute-start(f32[130,384]{1,0:T(8,128)S(1)} %pad_maximum_fusion.16), channel_id=1, source_target_pairs={{0,4},{4,0},{8,12},{12,8},{16,20},{20,16},{24,28},{28,24},{1,5},{5... | collective-permute-start | bytes 599048 | tf_op jit(solution)/shard_map/ppermute | solution.py:546
  484.6 35.1 %collective-permute-start.26 = (bf16[512,768]{1,0:T(8,128)(2,1)S(1)}, bf16[512,768]{1,0:T(8,128)(2,1)S(1)}, u32[]{:S(2)}, u32[]{:S(2)}) collective-permute-start(bf16[512,768]{1,0:T(8,128)(2,1)S(1)} %get-tuple-element.311), channel_id=1, source_target_pairs={{0,1},{1,0},{2,3},{3,2},{4,5},{5,4},{6,7},{7,6},{8,9},{9,8},{10,11... | collective-permute-start | bytes 2359304 | tf_op jit(solution)/shard_map/ppermute | solution.py:540
  495.0 24.9 %collective-permute-start.30 = (bf16[512,768]{1,0:T(8,128)(2,1)S(1)}, bf16[512,768]{1,0:T(8,128)(2,1)S(1)}, u32[]{:S(2)}, u32[]{:S(2)}) collective-permute-start(bf16[512,768]{1,0:T(8,128)(2,1)S(1)} %get-tuple-element.312), channel_id=1, source_target_pairs={{0,1},{1,0},{2,3},{3,2},{4,5},{5,4},{6,7},{7,6},{8,9},{9,8},{10,11... | collective-permute-start | bytes 2359304 | tf_op jit(solution)/shard_map/ppermute | solution.py:540
  498.6 18.4 %collective-permute-start.50 = (f32[130,384]{1,0:T(8,128)S(1)}, f32[130,384]{1,0:T(8,128)S(1)}, u32[]{:S(2)}, u32[]{:S(2)}) collective-permute-start(f32[130,384]{1,0:T(8,128)S(1)} %add.353), channel_id=1, source_target_pairs={{0,16},{4,20},{8,24},{12,28},{16,0},{20,4},{24,8},{28,12},{1,17},{... | collective-permute-start | bytes 599048 | tf_op jit(solution)/shard_map/ppermute | solution.py:546
  (114 other events, 890.5 us)
Sparse Core Ops, SparseCore 0:
  10.8 83.3 all-gather.5
  97.0 50.2 all-gather.3
